TPU v7x, 32 devices: a whole 2x2x4 slice. The times are simulated.
32 devices in a mesh: dp: 8 (over z, y), seq: 4 (over x, core).
Axes of the slice: x: 2, y: 2, z: 4, core: 2. Of those that a mesh axis runs over, the one named last changes fastest.
Arguments:
- tokens: bfloat16 [128, 1024, 1280], P('dp', 'seq'), may hold values from -6 to 6
- cotangent: bfloat16 [128, 1024, 1280], P('dp', 'seq'), may hold values from -6 to 6
- ln1_gain: bfloat16 [1280], replicated, may hold values from 0.25 to 1.75
- ln1_bias: bfloat16 [1280], replicated, may hold values from -3 to 3
- w_in: bfloat16 [1280, 640], replicated, may hold values from -0.15625 to 0.15625
- b_in: bfloat16 [640], replicated, may hold values from -3 to 3
- ln2_gain: bfloat16 [640], replicated, may hold values from 0.25 to 1.75
- ln2_bias: bfloat16 [640], replicated, may hold values from -3 to 3
- w_conv: bfloat16 [5, 640, 640], replicated, may hold values from -0.109375 to 0.109375
- b_conv: bfloat16 [640], replicated, may hold values from -3 to 3
- ln3_gain: bfloat16 [640], replicated, may hold values from 0.25 to 1.75
- ln3_bias: bfloat16 [640], replicated, may hold values from -3 to 3
- w_out: bfloat16 [640, 1280], replicated, may hold values from -0.3125 to 0.3125
- b_out: bfloat16 [1280], replicated, may hold values from -3 to 3
- lengths: int32 [128], P('dp'), may hold values from 64 to 1024, as said below
- offsets: int32 [128], P('dp'), may hold values from 0 to 960, as said below
- live: int32 [8], P('dp'), may hold values from 8 to 16, as said below
Outputs:
- output: bfloat16 [128, 1024, 1280], P('dp', 'seq')
- grad_tokens: bfloat16 [128, 1024, 1280], P('dp', 'seq')
- grad_ln1_gain: float32 [1280], replicated
- grad_ln1_bias: float32 [1280], replicated
- grad_w_in: float32 [1280, 640], replicated
- grad_b_in: float32 [640], replicated
- grad_ln2_gain: float32 [640], replicated
- grad_ln2_bias: float32 [640], replicated
- grad_w_conv: float32 [5, 640, 640], replicated
- grad_b_conv: float32 [640], replicated
- grad_ln3_gain: float32 [640], replicated
- grad_ln3_bias: float32 [640], replicated
- grad_w_out: float32 [640, 1280], replicated
- grad_b_out: float32 [1280], replicated
Inputs may be any that keep to these rules, and one draw needn't show every extreme that they name: offsets[s] + lengths[s] <= 1024. offsets[s] + lengths[s] <= 1024. Group g holds sequences in its slots 0 .. live[g] - 1; some group has all 16 slots filled.
All inputs are finite; a program needn't handle non-finite values.
Results may differ from a plain program's by a relative error of at most 0.0074.
Values may be sent and summed in bfloat16 or wider, within the bound.
A program may use at most 384 MiB of HBM per device.

v0:
```python
import jax
import jax.numpy as jnp
from jax import lax
from jax.sharding import PartitionSpec as P

KERNEL_TAPS = 5
DILATION_STEP = 128


EPSILON = 1e-05
SQRT_HALF = 0.7071067811865476
INV_ROOT_TAU = 0.3989422804014327


def normalize(values):
    centre = values - jnp.mean(values, axis=-1, keepdims=True)
    scale_inv = lax.rsqrt(jnp.mean(centre * centre, axis=-1, keepdims=True) + EPSILON)
    return (centre * scale_inv, scale_inv)


def gelu_exact(values):
    return jax.nn.gelu(values, approximate=False)


def gelu_slope(values):
    return 0.5 * (1.0 + lax.erf(values * SQRT_HALF)) + values * INV_ROOT_TAU * jnp.exp(
        -0.5 * values * values
    )


def norm_back(grad_out, normed, scale_inv, gain):
    grad_gain = jnp.sum(grad_out * normed, axis=0)
    grad_bias = jnp.sum(grad_out, axis=0)
    scaled = grad_out * gain
    grad_in = scale_inv * (
        scaled
        - jnp.mean(scaled, axis=-1, keepdims=True)
        - normed * jnp.mean(scaled * normed, axis=-1, keepdims=True)
    )
    return (grad_in, grad_gain, grad_bias)


def row_dot(left, right):
    return jnp.dot(left, right, preferred_element_type=jnp.float32)


def back_dot(left, right):
    return lax.dot_general(
        left, right, (((1,), (1,)), ((), ())), preferred_element_type=jnp.float32
    )


def column_dot(left, right):
    return lax.dot_general(
        left, right, (((0,), (0,)), ((), ())), preferred_element_type=jnp.float32
    )


def tap_stack(values, tap_offset, direction):
    receptive_rows = (KERNEL_TAPS - 1) // 2 * tap_offset
    padded_tokens = jnp.pad(values, ((0, 0), (receptive_rows, receptive_rows), (0, 0)))
    row_count = values.shape[1]
    pieces = []
    for kernel_tap_index in range(KERNEL_TAPS):
        begin = (
            receptive_rows + direction * (kernel_tap_index - (KERNEL_TAPS - 1) // 2) * tap_offset
        )
        pieces.append(padded_tokens[:, begin : begin + row_count])
    return jnp.concatenate(pieces, axis=-1)


def deal_shape(values, sequence_count):
    return values.reshape(
        values.shape[0], values.shape[1] // sequence_count, sequence_count, values.shape[2]
    )


def undeal_shape(values, sequence_count):
    return values.reshape(
        values.shape[0], sequence_count, values.shape[1] // sequence_count, 1, values.shape[2]
    )


def front_pass(tokens_in, keep_mask, ln1_gain, ln1_bias, w_in, b_in, ln2_gain, ln2_bias):
    slot_count, row_count, feat_width = tokens_in.shape
    normed_one, inv_one = normalize(tokens_in.reshape(-1, feat_width).astype(jnp.float32))
    pre_one = normed_one * ln1_gain.astype(jnp.float32) + ln1_bias.astype(jnp.float32)
    act_one = gelu_exact(pre_one).astype(jnp.bfloat16)
    hidden = row_dot(act_one, w_in) + b_in.astype(jnp.float32)
    normed_two, inv_two = normalize(hidden)
    pre_two = normed_two * ln2_gain.astype(jnp.float32) + ln2_bias.astype(jnp.float32)
    conv_in = (gelu_exact(pre_two).reshape(slot_count, row_count, -1) * keep_mask).astype(
        jnp.bfloat16
    )
    return (conv_in, (normed_one, inv_one, pre_one, act_one, normed_two, inv_two, pre_two))


def conv_forward(conv_in, w_conv, b_conv, tap_offset):
    stacked = tap_stack(conv_in, tap_offset, 1)
    flat_taps = stacked.reshape(-1, stacked.shape[-1])
    conv_out = (
        row_dot(flat_taps, w_conv.reshape(-1, w_conv.shape[2])) + b_conv.astype(jnp.float32)
    ).astype(jnp.bfloat16)
    return (conv_out.reshape(conv_in.shape[0], conv_in.shape[1], -1), flat_taps)


def rear_pass(conv_out, tokens_in, ln3_gain, ln3_bias, w_out, b_out):
    feat_width = tokens_in.shape[2]
    normed_three, inv_three = normalize(conv_out.reshape(-1, conv_out.shape[2]).astype(jnp.float32))
    pre_three = normed_three * ln3_gain.astype(jnp.float32) + ln3_bias.astype(jnp.float32)
    act_three = gelu_exact(pre_three).astype(jnp.bfloat16)
    summed = tokens_in.reshape(-1, feat_width).astype(jnp.float32) + (
        row_dot(act_three, w_out) + b_out.astype(jnp.float32)
    )
    return (
        summed.astype(jnp.bfloat16).reshape(tokens_in.shape),
        (normed_three, inv_three, pre_three, act_three),
    )


def rear_back(grad_output, kept_rear, ln3_gain, w_out):
    normed_three, inv_three, pre_three, act_three = kept_rear
    slot_count, row_count, feat_width = grad_output.shape
    grad_flat = grad_output.reshape(-1, feat_width)
    grad_low = grad_flat.astype(jnp.bfloat16)
    grad_w_out = column_dot(act_three, grad_low)
    grad_b_out = jnp.sum(grad_flat, axis=0)
    grad_pre = back_dot(grad_low, w_out) * gelu_slope(pre_three)
    grad_conv, grad_ln3_gain, grad_ln3_bias = norm_back(
        grad_pre, normed_three, inv_three, ln3_gain.astype(jnp.float32)
    )
    grad_conv = grad_conv.astype(jnp.bfloat16)
    grad_b_conv = jnp.sum(grad_conv, axis=0, dtype=jnp.float32)
    return (
        grad_conv.reshape(slot_count, row_count, -1),
        (grad_ln3_gain, grad_ln3_bias, grad_w_out, grad_b_out, grad_b_conv),
    )


def conv_back(grad_conv, flat_taps, w_conv, keep_mask, tap_offset):
    slot_count, row_count, inner_width = grad_conv.shape
    grad_taps = tap_stack(grad_conv, tap_offset, -1)
    flipped = jnp.transpose(w_conv, (0, 2, 1)).reshape(-1, w_conv.shape[1])
    grad_in = row_dot(grad_taps.reshape(-1, grad_taps.shape[-1]), flipped).reshape(
        slot_count, row_count, -1
    )
    grad_in = (grad_in * keep_mask).astype(jnp.bfloat16)
    grad_w_conv = column_dot(flat_taps, grad_conv.reshape(-1, inner_width)).reshape(w_conv.shape)
    return (grad_in, grad_w_conv)


def front_back(grad_conv_in, kept_front, grad_output, ln1_gain, w_in, ln2_gain):
    normed_one, inv_one, pre_one, act_one, normed_two, inv_two, pre_two = kept_front
    feat_width = grad_output.shape[2]
    grad_pre = grad_conv_in.reshape(-1, grad_conv_in.shape[2]).astype(jnp.float32) * gelu_slope(
        pre_two
    )
    grad_hidden, grad_ln2_gain, grad_ln2_bias = norm_back(
        grad_pre, normed_two, inv_two, ln2_gain.astype(jnp.float32)
    )
    grad_hidden = grad_hidden.astype(jnp.bfloat16)
    grad_b_in = jnp.sum(grad_hidden, axis=0, dtype=jnp.float32)
    grad_w_in = column_dot(act_one, grad_hidden)
    grad_first = back_dot(grad_hidden, w_in) * gelu_slope(pre_one)
    grad_branch, grad_ln1_gain, grad_ln1_bias = norm_back(
        grad_first, normed_one, inv_one, ln1_gain.astype(jnp.float32)
    )
    grad_tokens = (
        (grad_output.reshape(-1, feat_width) + grad_branch)
        .astype(jnp.bfloat16)
        .reshape(grad_output.shape)
    )
    return (
        grad_tokens,
        (grad_ln1_gain, grad_ln1_bias, grad_w_in, grad_b_in, grad_ln2_gain, grad_ln2_bias),
    )


def body(
    tokens,
    cotangent,
    ln1_gain,
    ln1_bias,
    w_in,
    b_in,
    ln2_gain,
    ln2_bias,
    w_conv,
    b_conv,
    ln3_gain,
    ln3_bias,
    w_out,
    b_out,
    lengths,
    offsets,
    live,
):
    sequence_count = lax.axis_size("seq")
    seq_index = lax.axis_index("seq")
    slot_count, row_count, feat_width = tokens.shape
    tap_offset = DILATION_STEP // sequence_count
    filled = jnp.arange(slot_count, dtype=jnp.int32) < live[0]
    ends = offsets + lengths
    local_rows = jnp.arange(row_count, dtype=jnp.int32)
    places = local_rows * sequence_count + seq_index
    inside = (places[None, :] >= offsets[:, None]) & (places[None, :] < ends[:, None])
    dealt_mask = (inside & filled[:, None]).astype(jnp.float32)[:, :, None]
    dealt_tokens, dealt_cot = (
        lax.all_to_all(
            deal_shape(tokens, sequence_count), "seq", split_axis=2, concat_axis=1, tiled=True
        ),
        lax.all_to_all(
            deal_shape(cotangent, sequence_count), "seq", split_axis=2, concat_axis=1, tiled=True
        ),
    )
    dealt_tokens = dealt_tokens.reshape(slot_count, row_count, -1)
    dealt_cot = dealt_cot.reshape(slot_count, row_count, -1)
    conv_in, kept_front = front_pass(
        dealt_tokens, dealt_mask, ln1_gain, ln1_bias, w_in, b_in, ln2_gain, ln2_bias
    )
    conv_out, flat_taps = conv_forward(conv_in, w_conv, b_conv, tap_offset)
    dealt_output, kept_rear = rear_pass(conv_out, dealt_tokens, ln3_gain, ln3_bias, w_out, b_out)
    grad_output = dealt_cot.astype(jnp.float32) * dealt_mask
    grad_conv, rear_grads = rear_back(grad_output, kept_rear, ln3_gain, w_out)
    grad_conv_in, grad_w_conv = conv_back(grad_conv, flat_taps, w_conv, dealt_mask, tap_offset)
    dealt_grad, front_grads = front_back(
        grad_conv_in, kept_front, grad_output, ln1_gain, w_in, ln2_gain
    )
    output, grad_tokens = (
        lax.all_to_all(
            undeal_shape(dealt_output, sequence_count),
            "seq",
            split_axis=1,
            concat_axis=3,
            tiled=True,
        ),
        lax.all_to_all(
            undeal_shape(dealt_grad, sequence_count), "seq", split_axis=1, concat_axis=3, tiled=True
        ),
    )
    output = output.reshape(slot_count, row_count, feat_width)
    grad_tokens = grad_tokens.reshape(slot_count, row_count, feat_width)
    grad_ln1_gain, grad_ln1_bias, grad_w_in, grad_b_in, grad_ln2_gain, grad_ln2_bias = front_grads
    grad_ln3_gain, grad_ln3_bias, grad_w_out, grad_b_out, grad_b_conv = rear_grads
    summed = lax.psum(
        (
            grad_ln1_gain,
            grad_ln1_bias,
            grad_w_in,
            grad_b_in,
            grad_ln2_gain,
            grad_ln2_bias,
            grad_w_conv,
            grad_b_conv,
            grad_ln3_gain,
            grad_ln3_bias,
            grad_w_out,
            grad_b_out,
        ),
        ("dp", "seq"),
    )
    return (output, grad_tokens) + tuple(summed)


def solution(mesh):
    return jax.shard_map(
        body,
        mesh=mesh,
        in_specs=(
            P("dp", "seq", None),
            P("dp", "seq", None),
            P(),
            P(),
            P(),
            P(),
            P(),
            P(),
            P(),
            P(),
            P(),
            P(),
            P(),
            P(),
            P("dp"),
            P("dp"),
            P("dp"),
        ),
        out_specs=(
            P("dp", "seq", None),
            P("dp", "seq", None),
            P(),
            P(),
            P(),
            P(),
            P(),
            P(),
            P(),
            P(),
            P(),
            P(),
            P(),
            P(),
        ),
        check_vma=False,
    )
```

profile of v0, /device:TPU:0, one launch (start us, length us, event | category | flops | bytes accessed | tf_op | source)
XLA Modules:
  0.0 1063.2 jit_solution(446926403261814694)
XLA Ops:
  7.2 14.0 %copy.63 = bf16[16,256,1280]{2,0,1:T(8,128)(2,1)} copy(bf16[16,256,1280]{2,1,0:T(8,128)(2,1)} %param.17) | data formatting | bytes 20971520 | tf_op args[0]
  21.2 14.1 %copy.64 = bf16[16,64,4,1280]{3,1,0,2:T(8,128)(2,1)} copy(bf16[16,64,4,1280]{3,0,2,1:T(8,128)(2,1)} %bitcast.116) | data formatting | bytes 20971520 | tf_op jit(solution)/shard_map/reshape | solution.py:73
  42.6 13.9 %copy.70 = bf16[16,256,1280]{2,0,1:T(8,128)(2,1)} copy(bf16[16,256,1280]{2,1,0:T(8,128)(2,1)} %param.18) | data formatting | bytes 20971520 | tf_op args[1]
  56.6 13.9 %copy.71 = bf16[16,64,4,1280]{3,1,0,2:T(8,128)(2,1)} copy(bf16[16,64,4,1280]{3,0,2,1:T(8,128)(2,1)} %bitcast.117) | data formatting | bytes 20971520 | tf_op jit(solution)/shard_map/reshape | solution.py:73
  80.8 76.9 %all-to-all-done = bf16[16,64,4,1280]{3,1,0,2:T(8,128)(2,1)} async-done(((bf16[16,64,4,1280]{3,1,0,2:T(8,128)(2,1)}), bf16[16,64,4,1280]{3,1,0,2:T(8,128)(2,1)}, u32[]{:S(2)}, u32[]{:S(2)}) %all-to-all-start) | async-done | bytes 10485792 | tf_op jit(solution)/shard_map/all_to_all | solution.py:209
  176.3 13.9 %convert_bitcast_fusion.1 = f32[16,4,64,1,1280]{4,2,0,1,3:T(8,128)} fusion(bf16[16,64,4,1280]{3,1,0,2:T(8,128)(2,1)} %all-to-all-done), kind=kLoop, calls=%fused_computation.11 | loop fusion | flops 5242880 | bytes 31457280 | tf_op jit(solution)/shard_map/convert_element_type | solution.py:112
  190.2 16.3 %copy.65 = f32[16,4,64,1,1280]{4,2,1,0,3:T(8,128)} copy(f32[16,4,64,1,1280]{4,2,0,1,3:T(8,128)} %convert_bitcast_fusion.1) | data formatting | bytes 41943040 | tf_op jit(solution)/shard_map/convert_element_type | solution.py:112
  206.6 56.4 %fusion.7 = (f32[4096,1280]{1,0:T(8,128)}, bf16[4096,1280]{1,0:T(8,128)(2,1)}) fusion(f32[16,4,64,1,1280]{4,2,1,0,3:T(8,128)} %copy.65, f32[4096]{0:T(1024)S(1)} %rsqrt.28, f32[4096]{0:T(1024)S(1)} %div.39, f32[1280]{0:T(1024)S(1)} %convert_element_type.134, f32[1280]{0:T(1024)S(1)} %convert_element_type.133), kind=kLoop, calls=%fused_computation.14 | loop fusion | flops 361758720 | bytes 52471808 | tf_op jit(solution)/shard_map/mul | solution.py:18
  263.0 11.8 %add_reduce_fusion = (f32[4096]{0:T(1024)S(1)}, f32[4096,640]{1,0:T(8,128)S(1)}) fusion(f32[640]{0:T(1024)S(1)} %convert_element_type.136, bf16[4096,1280]{1,0:T(8,128)(2,1)} %get-tuple-element.72, bf16[1280,640]{1,0:T(8,128)(2,1)S(1)} %copy-done), kind=kOutput, calls=%fused_computation.123 | convolution fusion | flops 6716125184 | bytes 22628864 | tf_op jit(solution)/shard_map/dot_general | solution.py:44
  277.1 29.4 %fusion.44 = f32[4096,640]{1,0:T(8,128)} fusion(f32[640]{0:T(1024)S(1)} %convert_element_type.138, f32[640]{0:T(1024)S(1)} %convert_element_type.137, f32[4096]{0:T(1024)S(1)} %add_rsqrt_fusion.2, f32[4096]{0:T(1024)S(1)} %broadcast_multiply_fusion.8, f32[4096,640]{1,0:T(8,128)S(1)} %get-tuple-element.75, f32[640]{0:T(1024)S(1)} %convert_element_type.136), kind=kLoop, calls=%fused_computation.72 | loop fusion | flops 180879360 | bytes 21011968 | tf_op jit(solution)/shard_map/mul | solution.py:22
  330.9 24.9 %convert_reduce_fusion = (f32[4096]{0:T(1024)S(1)}, bf16[4096,640]{1,0:T(8,128)(2,1)S(1)}) fusion(f32[640]{0:T(1024)S(1)} %convert_element_type.141, bf16[4096,3200]{1,0:T(8,128)(2,1)} %bitcast.118, bf16[3200,640]{1,0:T(8,128)(2,1)S(1)} %bitcast.124), kind=kOutput, calls=%fused_computation.44 | convolution fusion | flops 16787697664 | bytes 35572224 | tf_op jit(solution)/shard_map/dot_general | solution.py:44
  360.3 13.9 %convert_bitcast_fusion = f32[16,4,64,1,1280]{4,2,0,1,3:T(8,128)} fusion(bf16[16,64,4,1280]{3,1,0,2:T(8,128)(2,1)} %all-to-all-done.2), kind=kLoop, calls=%fused_computation.9 | loop fusion | flops 5242880 | bytes 31457280 | tf_op jit(solution)/shard_map/convert_element_type | solution.py:223
  374.1 16.4 %copy.72 = f32[16,4,64,1,1280]{4,2,1,0,3:T(8,128)} copy(f32[16,4,64,1,1280]{4,2,0,1,3:T(8,128)} %convert_bitcast_fusion) | data formatting | bytes 41943040 | tf_op jit(solution)/shard_map/convert_element_type | solution.py:223
  390.5 33.8 %copy.76 = bf16[3200,4096]{1,0:T(8,128)(2,1)} copy(bf16[3200,4096]{0,1:T(8,128)(2,1)} %bitcast.119) | data formatting | bytes 52428800 | tf_op jit(solution)/shard_map/dot_general | solution.py:54
  434.2 17.3 %fusion.41 = (f32[640]{0:T(1024)}, f32[4096]{0:T(1024)S(1)}, f32[4096]{0:T(1024)S(1)}, f32[640]{0:T(1024)}, f32[4096,640]{1,0:T(8,128)S(1)}) fusion(bf16[4096,640]{1,0:T(8,128)(2,1)} %copy-done.3, f32[4096]{0:T(1024)S(1)} %add_rsqrt_fusion.1, f32[4096]{0:T(1024)S(1)} %broadcast_multiply_fusion.7, f32[640]{0:T(1024)S(1)} %copy-done.31, ...), kind=kOutput, calls=%fused_computation.69 | convolution fusion | flops 6765927424 | bytes 27928576 | tf_op jit(solution)/shard_map/dot_general | solution.py:48
  451.5 46.2 %convert_reduce_fusion.1 = (f32[640]{0:T(1024)}, bf16[4096,640]{1,0:T(8,128)(2,1)S(1)}, bf16[4096,640]{1,0:T(8,128)(2,1)}) fusion(f32[4096]{0:T(1024)S(1)} %get-tuple-element.80, f32[4096]{0:T(1024)S(1)} %broadcast_multiply_fusion.7, bf16[4096,640]{1,0:T(8,128)(2,1)S(1)} %bitcast.122, f32[4096]{0:T(1024)S(1)} %get-tuple-element.81, ...), kind=kLoop, calls=%fused_computation.80 | loop fusion | flops 204471680 | bytes 26287616 | tf_op jit(solution)/shard_map/reduce_sum | solution.py:133
  513.7 25.8 %multiply_convert_fusion.1 = bf16[16,256,640]{2,1,0:T(8,128)(2,1)S(1)} fusion(f32[16,256]{1,0:T(8,128)S(1)} %and_convert_fusion.2, bf16[16,256,3200]{2,1,0:T(8,128)(2,1)} %fusion.75, bf16[3200,640,1]{1,0,2:T(8,128)(2,1)} %bitcast.125), kind=kOutput, calls=%fused_computation.85 | convolution fusion | flops 16782458880 | bytes 35569664 | tf_op jit(solution)/shard_map/dot_general | solution.py:44
  539.6 14.1 %multiply_reduce_fusion.5 = (f32[640]{0:T(1024)}, f32[4096]{0:T(1024)S(1)}, f32[4096]{0:T(1024)S(1)}, f32[640]{0:T(1024)}, f32[4096,640]{1,0:T(8,128)}) fusion(f32[4096]{0:T(1024)S(1)} %copy-done.11, f32[4096]{0:T(1024)S(1)} %copy-done.9, f32[4096,640]{1,0:T(8,128)S(1)} %bitcast.110, f32[640]{0:T(1024)S(1)} %copy-done.18, f32[640]{0:T(1024)S(1)} %copy-done.22, ...), kind=kLoop, calls=%fused_computation.81 | loop fusion | flops 57662208 | bytes 26292736 | tf_op jit(solution)/shard_map/reduce_sum | solution.py:32
  553.8 10.1 convert_reduce_fusion.2
  564.0 27.6 %multiply_reduce_fusion.1 = (f32[1280]{0:T(1024)S(1)}, f32[4096]{0:T(1024)S(1)}, f32[4096]{0:T(1024)S(1)}, f32[1280]{0:T(1024)S(1)}, f32[4096,1280]{1,0:T(8,128)}) fusion(f32[16,4,64,1,1280]{4,2,1,0,3:T(8,128)S(1)} %bitcast.108, f32[4096]{0:T(1024)S(1)} %copy-done.14, f32[4096]{0:T(1024)S(1)} %copy-done.16, f32[1280]{0:T(1024)S(1)} %copy-done.20, ...), kind=kOutput, calls=%fused_computation.17 | convolution fusion | flops 6815733760 | bytes 69881856 | tf_op jit(solution)/shard_map/dot_general | solution.py:48
  591.6 25.1 %add_convert_fusion = bf16[4096,1280]{1,0:T(8,128)(2,1)} fusion(f32[16,4,64,1,1280]{4,2,1,0,3:T(8,128)} %copy.72, f32[4096,1280]{1,0:T(8,128)} %get-tuple-element.79, f32[16,4,64,1,1280]{4,2,1,0,3:T(8,128)} %copy.65, f32[4096]{0:T(1024)S(1)} %broadcast_multiply_fusion.1, f32[4096]{0:T(1024)S(1)} %broadcast_multiply_fusion.2, f32[4096]{0:T(1024)S(1)} %copy-done.12, ...), kind=kLoop, calls=%fused_computation.18 | loop fusion | flops 52428800 | bytes 73487360 | tf_op jit(solution)/shard_map/convert_element_type | solution.py:170
  632.1 16.1 %fusion.8 = bf16[4096,1280]{1,0:T(8,128)(2,1)} fusion(f32[16,4,64,1,1280]{4,2,1,0,3:T(8,128)} %copy.65, bf16[4096,640]{1,0:T(8,128)(2,1)} %get-tuple-element.73, bf16[640,1280]{1,0:T(8,128)(2,1)} %param.29, f32[1280]{0:T(1024)S(1)} %copy-done.33), kind=kOutput, calls=%fused_computation.15 | convolution fusion | flops 6726615040 | bytes 38343680 | tf_op jit(solution)/shard_map/dot_general | solution.py:44
  657.4 13.9 %fusion.80 = f32[1280,640]{1,0:T(8,128)} fusion(bf16[4096,1280]{1,0:T(8,128)(2,1)} %get-tuple-element.72, bf16[4096,640]{1,0:T(8,128)(2,1)} %copy-done.5), kind=kOutput, calls=%fused_computation.164 | convolution fusion | flops 6710886400 | bytes 19005440 | tf_op jit(solution)/shard_map/dot_general | solution.py:54
  671.4 25.3 %fusion.76 = f32[5,640,640]{2,1,0:T(8,128)} fusion(bf16[5,640,4096]{2,1,0:T(8,128)(2,1)} %bitcast.120, bf16[4096,640]{1,0:T(8,128)(2,1)S(1)} %bitcast.106), kind=kOutput, calls=%fused_computation.140 | convolution fusion | flops 16777216000 | bytes 39649280 | tf_op jit(solution)/shard_map/dot_general | solution.py:54
  696.7 51.0 %all-to-all-done.3 = bf16[16,4,64,1,1280]{4,2,0,3,1:T(8,128)(2,1)} async-done(((bf16[16,4,64,1,1280]{4,2,0,3,1:T(8,128)(2,1)}), bf16[16,4,64,1,1280]{4,2,0,3,1:T(8,128)(2,1)}, u32[]{:S(2)}, u32[]{:S(2)}) %all-to-all-start.3) | async-done | bytes 10485792 | tf_op jit(solution)/shard_map/all_to_all | solution.py:237
  753.7 12.3 %fusion.81 = f32[640,1280]{1,0:T(8,128)} fusion(bf16[4096,640]{1,0:T(8,128)(2,1)} %get-tuple-element.73, bf16[4096,1280]{1,0:T(8,128)(2,1)} %copy-done.4), kind=kOutput, calls=%fused_computation.165 | convolution fusion | flops 6710886400 | bytes 19005440 | tf_op jit(solution)/shard_map/dot_general | solution.py:54
  772.9 175.7 %all-reduce.2 = (f32[1280]{0:T(1024)}, f32[1280]{0:T(1024)}, f32[640]{0:T(1024)}, f32[640]{0:T(1024)}, f32[640]{0:T(1024)}, /*index=5*/f32[640]{0:T(1024)}, f32[640]{0:T(1024)}, f32[640]{0:T(1024)}, f32[1280]{0:T(1024)}) all-reduce(f32[1280]{0:T(1024)S(1)} %get-tuple-element.42, ...), channel_id=1, replica_groups=mesh['dp'=8,'seq'=4] {'dp','seq'}, use_global_device_ids=true, to_apply=%region_13.14 | all-reduce | flops 7680 | bytes 61440 | tf_op jit(solution)/shard_map/psum | solution.py:245
  948.5 13.9 %copy.75 = bf16[16,4,64,1,1280]{4,0,1,2,3:T(8,128)(2,1)} copy(bf16[16,4,64,1,1280]{4,2,0,3,1:T(8,128)(2,1)} %all-to-all-done.3) | data formatting | bytes 20971520 | tf_op jit(solution)/shard_map/all_to_all | solution.py:237
  962.5 11.6 %copy.78 = bf16[16,256,1280]{2,1,0:T(8,128)(2,1)} copy(bf16[16,256,1280]{2,0,1:T(8,128)(2,1)} %bitcast.114) | data formatting | bytes 20971520
  974.1 14.3 %copy.69 = bf16[16,4,64,1,1280]{4,0,1,2,3:T(8,128)(2,1)} copy(bf16[16,4,64,1,1280]{4,2,0,3,1:T(8,128)(2,1)} %all-to-all-done.1) | data formatting | bytes 20971520 | tf_op jit(solution)/shard_map/all_to_all | solution.py:230
  988.4 11.7 %copy.77 = bf16[16,256,1280]{2,1,0:T(8,128)(2,1)} copy(bf16[16,256,1280]{2,0,1:T(8,128)(2,1)} %bitcast.115) | data formatting | bytes 20971520
  1000.1 43.0 %all-reduce.6.cloned.1.call-done = (f32[1280,640]{1,0:T(8,128)}, f32[5,640,640]{2,1,0:T(8,128)}, f32[640,1280]{1,0:T(8,128)}) async-done(((f32[1280,640]{1,0:T(8,128)}, f32[5,640,640]{2,1,0:T(8,128)}, f32[640,1280]{1,0:T(8,128)}), (f32[1280,640]{1,0:T(8,128)}, f32[5,640,640]{2,1,0:T(8,128)}, f32[640,1280]{1,0:T(8,128)})) %all-reduce.6.cloned.1.call-update) | async-done | bytes 14745616 | tf_op jit(solution)/shard_map/psum | solution.py:245
  (203 shorter events, 142.4 us)
Async XLA Ops:
  7.2 255.8 %copy-start = (bf16[1280,640]{1,0:T(8,128)(2,1)S(1)}, bf16[1280,640]{1,0:T(8,128)(2,1)}, u32[]{:S(2)}) copy-start(bf16[1280,640]{1,0:T(8,128)(2,1)} %param.21) | copy-start | bytes 4915204
  35.4 122.4 %all-to-all-start = ((bf16[16,64,4,1280]{3,1,0,2:T(8,128)(2,1)}), bf16[16,64,4,1280]{3,1,0,2:T(8,128)(2,1)}, u32[]{:S(2)}, u32[]{:S(2)}) async-start(bf16[16,64,4,1280]{3,1,0,2:T(8,128)(2,1)} %copy.64), calls=%async_computation | async-start | bytes 20971520 | tf_op jit(solution)/shard_map/all_to_all | solution.py:209
  41.5 165.0 %copy-start.19 = (f32[1280]{0:T(1024)}, f32[1280]{0:T(1024)S(1)}, u32[]{:S(2)}) copy-start(f32[1280]{0:T(1024)S(1)} %convert_element_type.133) | copy-start | bytes 15364
  41.5 165.0 %copy-start.25 = (f32[1280]{0:T(1024)}, f32[1280]{0:T(1024)S(1)}, u32[]{:S(2)}) copy-start(f32[1280]{0:T(1024)S(1)} %convert_element_type.134) | copy-start | bytes 15364
  41.6 235.5 %copy-start.17 = (f32[640]{0:T(1024)}, f32[640]{0:T(1024)S(1)}, u32[]{:S(2)}) copy-start(f32[640]{0:T(1024)S(1)} %convert_element_type.136) | copy-start | bytes 7684
  41.6 235.5 %copy-start.21 = (f32[640]{0:T(1024)}, f32[640]{0:T(1024)S(1)}, u32[]{:S(2)}) copy-start(f32[640]{0:T(1024)S(1)} %convert_element_type.137) | copy-start | bytes 7684
  41.6 235.5 %copy-start.23 = (f32[640]{0:T(1024)}, f32[640]{0:T(1024)S(1)}, u32[]{:S(2)}) copy-start(f32[640]{0:T(1024)S(1)} %convert_element_type.138) | copy-start | bytes 7684
  42.3 37.8 %copy-start.36 = (s32[16]{0:T(128)}, s32[16]{0:T(128)S(1)}, u32[]{:S(2)}) copy-start(s32[16]{0:T(128)S(1)} %add.154) | copy-start | bytes 196
  42.4 37.7 %copy-start.38 = (pred[16]{0:T(512)(128)(4,1)}, pred[16]{0:T(512)(128)(4,1)S(1)}, u32[]{:S(2)}) copy-start(pred[16]{0:T(512)(128)(4,1)S(1)} %iota_compare_fusion) | copy-start | bytes 52
  157.8 202.5 %all-to-all-start.2 = ((bf16[16,64,4,1280]{3,1,0,2:T(8,128)(2,1)}), bf16[16,64,4,1280]{3,1,0,2:T(8,128)(2,1)}, u32[]{:S(2)}, u32[]{:S(2)}) async-start(bf16[16,64,4,1280]{3,1,0,2:T(8,128)(2,1)} %copy.71), calls=%async_computation.2 | async-start | bytes 20971520 | tf_op jit(solution)/shard_map/all_to_all | solution.py:212
  176.3 30.3 %copy-start.13 = (f32[4096]{0:T(1024)}, f32[4096]{0:T(1024)S(1)}, u32[]{:S(2)}) copy-start(f32[4096]{0:T(1024)S(1)} %rsqrt.28) | copy-start | bytes 49156
  206.5 56.5 %copy-start.15 = (f32[4096]{0:T(1024)}, f32[4096]{0:T(1024)S(1)}, u32[]{:S(2)}) copy-start(f32[4096]{0:T(1024)S(1)} %div.39) | copy-start | bytes 49156
  274.8 31.7 %copy-start.2 = (f32[4096,640]{1,0:T(8,128)}, f32[4096,640]{1,0:T(8,128)S(1)}, u32[]{:S(2)}) copy-start(f32[4096,640]{1,0:T(8,128)S(1)} %get-tuple-element.75) | copy-start | bytes 31457284
  274.8 31.6 %copy-start.8 = (f32[4096]{0:T(1024)}, f32[4096]{0:T(1024)S(1)}, u32[]{:S(2)}) copy-start(f32[4096]{0:T(1024)S(1)} %broadcast_multiply_fusion.8) | copy-start | bytes 49156
  277.1 29.4 %copy-start.10 = (f32[4096]{0:T(1024)}, f32[4096]{0:T(1024)S(1)}, u32[]{:S(2)}) copy-start(f32[4096]{0:T(1024)S(1)} %add_rsqrt_fusion.2) | copy-start | bytes 49156
  390.5 33.8 %copy-start.12 = (f32[4096]{0:T(1024)S(1)}, f32[4096]{0:T(1024)}, u32[]{:S(2)}) copy-start(f32[4096]{0:T(1024)} %and_convert_fusion.1) | copy-start | bytes 49156
  424.3 27.1 %slice-start.10 = ((s8[5242880]{0:T(1024)(128)(4,1)}), s8[4194304]{0:T(1024)(128)(4,1)S(1)}, s32[]{:S(2)}) async-start(s8[5242880]{0:T(1024)(128)(4,1)} %bitcast.121), calls=%async_computation.15 | async-start | bytes 8388608
  510.5 29.0 %slice-start.7 = ((s8[10485760]{0:T(1024)(128)(4,1)}), s8[4194304]{0:T(1024)(128)(4,1)S(1)}, s32[]{:S(2)}) async-start(s8[10485760]{0:T(1024)(128)(4,1)} %bitcast.109), calls=%async_computation.12 | async-start | bytes 8388608
  513.7 25.9 %slice-start.8 = ((s8[10485760]{0:T(1024)(128)(4,1)}), s8[4194304]{0:T(1024)(128)(4,1)S(1)}, s32[]{:S(2)}) async-start(s8[10485760]{0:T(1024)(128)(4,1)} %bitcast.109), calls=%async_computation.13 | async-start | bytes 8388608
  513.7 25.9 %slice-start.9 = ((s8[10485760]{0:T(1024)(128)(4,1)}), s8[2097152]{0:T(1024)(128)(4,1)S(1)}, s32[]{:S(2)}) async-start(s8[10485760]{0:T(1024)(128)(4,1)} %bitcast.109), calls=%async_computation.14 | async-start | bytes 4194304
  513.7 25.9 %copy-start.9 = (f32[4096]{0:T(1024)S(1)}, f32[4096]{0:T(1024)}, u32[]{:S(2)}) copy-start(f32[4096]{0:T(1024)} %copy-done.8) | copy-start | bytes 49156
  513.7 25.9 %copy-start.11 = (f32[4096]{0:T(1024)S(1)}, f32[4096]{0:T(1024)}, u32[]{:S(2)}) copy-start(f32[4096]{0:T(1024)} %copy-done.10) | copy-start | bytes 49156
  513.7 25.9 %copy-start.18 = (f32[640]{0:T(1024)S(1)}, f32[640]{0:T(1024)}, u32[]{:S(2)}) copy-start(f32[640]{0:T(1024)} %copy-done.17) | copy-start | bytes 7684
  513.7 25.9 %copy-start.22 = (f32[640]{0:T(1024)S(1)}, f32[640]{0:T(1024)}, u32[]{:S(2)}) copy-start(f32[640]{0:T(1024)} %copy-done.21) | copy-start | bytes 7684
  513.7 25.9 %copy-start.24 = (f32[640]{0:T(1024)S(1)}, f32[640]{0:T(1024)}, u32[]{:S(2)}) copy-start(f32[640]{0:T(1024)} %copy-done.23) | copy-start | bytes 7684
  539.6 24.3 %slice-start.2 = ((s8[20971520]{0:T(1024)(128)(4,1)}), s8[4194304]{0:T(1024)(128)(4,1)S(1)}, s32[]{:S(2)}) async-start(s8[20971520]{0:T(1024)(128)(4,1)} %bitcast.107), calls=%async_computation.7 | async-start | bytes 8388608
  539.6 24.3 %slice-start.3 = ((s8[20971520]{0:T(1024)(128)(4,1)}), s8[4194304]{0:T(1024)(128)(4,1)S(1)}, s32[]{:S(2)}) async-start(s8[20971520]{0:T(1024)(128)(4,1)} %bitcast.107), calls=%async_computation.8 | async-start | bytes 8388608
  539.6 24.3 %slice-start.4 = ((s8[20971520]{0:T(1024)(128)(4,1)}), s8[4194304]{0:T(1024)(128)(4,1)S(1)}, s32[]{:S(2)}) async-start(s8[20971520]{0:T(1024)(128)(4,1)} %bitcast.107), calls=%async_computation.9 | async-start | bytes 8388608
  563.9 27.7 %copy-start.5 = (bf16[4096,640]{1,0:T(8,128)(2,1)}, bf16[4096,640]{1,0:T(8,128)(2,1)S(1)}, u32[]{:S(2)}) copy-start(bf16[4096,640]{1,0:T(8,128)(2,1)S(1)} %get-tuple-element.69) | copy-start | bytes 15728644
  625.9 121.7 %all-to-all-start.3 = ((bf16[16,4,64,1,1280]{4,2,0,3,1:T(8,128)(2,1)}), bf16[16,4,64,1,1280]{4,2,0,3,1:T(8,128)(2,1)}, u32[]{:S(2)}, u32[]{:S(2)}) async-start(bf16[16,4,64,1,1280]{4,2,0,3,1:T(8,128)(2,1)} %copy.74), calls=%async_computation.3 | async-start | bytes 20971520 | tf_op jit(solution)/shard_map/all_to_all | solution.py:237
  747.7 226.4 %all-to-all-start.1 = ((bf16[16,4,64,1,1280]{4,2,0,3,1:T(8,128)(2,1)}), bf16[16,4,64,1,1280]{4,2,0,3,1:T(8,128)(2,1)}, u32[]{:S(2)}, u32[]{:S(2)}) async-start(bf16[16,4,64,1,1280]{4,2,0,3,1:T(8,128)(2,1)} %copy.68), calls=%async_computation.1 | async-start | bytes 20971520 | tf_op jit(solution)/shard_map/all_to_all | solution.py:230
  753.7 289.4 %all-reduce.6.cloned.1.call-start = ((), (), s32[]{:S(2)}) async-start(), calls=%async_computation.4 | async-start | bytes 29491200 | tf_op jit(solution)/shard_map/psum | solution.py:245
  (38 other events, 347.1 us)
Sparse Core Ops, SparseCore 0:
  766.2 276.7 all-reduce.5
where the time goes:
time: 1070 us; the launch traced here: 1060 us
  other arithmetic  256 us (24%)
  local copies, waits for them, and re-layouts  245 us (23%)
  blocking collectives  176 us (16%)
  matrix products  175 us (16%)
  waiting for transfers between devices  171 us (16%)
  starting transfers between devices  24.2 us (2%)
  between operations  16.1 us (2%)
    psum x1, blocking collectives, body(): lax.psum((grad_ln1_gain, grad_ln1_bias, grad_w_in, grad_b_in, grad_ln2_ga...  176 us
    unnamed x149, local copies, waits for them, and re-layouts  97.4 us
    dot_general x4, matrix products, row_dot(): return jnp.dot(left, right, preferred_element_type=jnp.float32)  78.7 us
    all_to_all x1, waiting for transfers between devices, body(): lax.all_to_all(deal_shape(tokens, sequence_count), 'seq', split_axis=2, c...  76.9 us
    mul x1, other arithmetic, normalize(): return (centre * scale_inv, scale_inv)  56.4 us
    dot_general x3, matrix products, column_dot(): lax.dot_general(left, right, (((0,), (0,)), ((), ())), preferred_element_...  51.5 us
    all_to_all x1, waiting for transfers between devices, body(): lax.all_to_all(undeal_shape(dealt_grad, sequence_count), 'seq', split_axi...  51 us
    reduce_sum x1, other arithmetic, rear_back(): grad_b_conv = jnp.sum(grad_conv, axis=0, dtype=jnp.float32)  46.2 us
  transfers between devices with their start and end apart: 5, of which 3 were waited for; matrix products, arithmetic and copies ran while one was open for 35% of the time, Pallas kernels for 0%

commit v1 on v0

v1 whole, which is shorter than its diff:
```python
import functools

import jax
import jax.numpy as jnp
from jax import lax
from jax.experimental import pallas as pl
from jax.experimental.pallas import tpu as pltpu
from jax.sharding import PartitionSpec as P

TAPS = 5
STEP = 128
REACH = (TAPS - 1) // 2 * STEP
EPSILON = 1e-05
SQRT_HALF = 0.7071067811865476
INV_ROOT_TAU = 0.3989422804014327
VMEM_LIMIT = 60 * 1024 * 1024
F32 = jnp.float32
BF16 = jnp.bfloat16


def dot(left, right):
    return jnp.dot(left, right, preferred_element_type=F32)


def dot_back(left, right):
    return lax.dot_general(left, right, (((1,), (1,)), ((), ())), preferred_element_type=F32)


def dot_rows(left, right):
    return lax.dot_general(left, right, (((0,), (0,)), ((), ())), preferred_element_type=F32)


def normalize(values):
    centre = values - jnp.mean(values, axis=-1, keepdims=True)
    inv = lax.rsqrt(jnp.mean(centre * centre, axis=-1, keepdims=True) + EPSILON)
    return centre * inv, inv


def gelu_pair(values):
    gate = 0.5 + 0.5 * lax.erf(values * SQRT_HALF)
    slope = gate + values * (INV_ROOT_TAU * jnp.exp(-0.5 * values * values))
    return values * gate, slope


def norm_back(grad, normed, inv, gain):
    scaled = grad * gain
    return inv * (
        scaled
        - jnp.mean(scaled, axis=-1, keepdims=True)
        - normed * jnp.mean(scaled * normed, axis=-1, keepdims=True)
    )


def keep_rows(win_ref, slot, shape):
    rows = lax.broadcasted_iota(jnp.int32, shape, 0)
    return (rows >= win_ref[0, slot]) & (rows < win_ref[1, slot])


def row_sum(values):
    return jnp.sum(values, axis=0, keepdims=True)


def spread(inv):
    return jnp.broadcast_to(inv, (inv.shape[0], 128))


def front_kernel(base, win, tok, g1, b1, w_in, b_in, g2, b2, h, a1, s1, n1, r1, s2, n2, r2):
    slot = base + pl.program_id(0)
    normed, inv = normalize(tok[0].astype(F32))
    n1[0] = normed.astype(BF16)
    r1[0] = spread(inv)
    act, slope = gelu_pair(normed * g1[...] + b1[...])
    act = act.astype(BF16)
    a1[0] = act
    s1[0] = slope.astype(BF16)
    hidden = dot(act, w_in[...]) + b_in[...]
    normed, inv = normalize(hidden)
    n2[0] = normed.astype(BF16)
    r2[0] = spread(inv)
    act, slope = gelu_pair(normed * g2[...] + b2[...])
    s2[0] = slope.astype(BF16)
    h[0] = jnp.where(keep_rows(win, slot, act.shape), act, 0.0).astype(BF16)


def rear_kernel(
    base, first, last, halves, rows, win, *refs
):
    pieces = refs[: 2 * halves + 1]
    refs = refs[2 * halves + 1 :]
    tok, cot, w_conv, b_conv, g3, b3, w_out, b_out = refs[:8]
    refs = refs[8:]
    if not first:
        wconv_in, wout_in, small_in = refs[:3]
        refs = refs[4:]
    out, dc_out, gw_conv, gw_out, small, acc_conv, acc_out, acc_small, strip = refs
    step = pl.program_id(0)

    @pl.when(step == 0)
    def _():
        if first:
            acc_conv[...] = jnp.zeros_like(acc_conv)
            acc_out[...] = jnp.zeros_like(acc_out)
            acc_small[...] = jnp.zeros_like(acc_small)
        else:
            acc_conv[...] = wconv_in[...]
            acc_out[...] = wout_in[...]
            acc_small[...] = small_in[...]

    slot = base + step
    at = 0
    for piece in pieces:
        count = piece.shape[1]
        strip[at : at + count] = piece[0]
        at += count
    inner = strip.shape[1]
    conv = dot(strip[0:rows], w_conv[0])
    for tap in range(1, TAPS):
        conv += dot(strip[tap * STEP : tap * STEP + rows], w_conv[tap])
    conv = (conv + b_conv[...]).astype(BF16).astype(F32)
    normed, inv = normalize(conv)
    act, slope = gelu_pair(normed * g3[...] + b3[...])
    act = act.astype(BF16)
    out[0] = (tok[0].astype(F32) + (dot(act, w_out[...]) + b_out[...])).astype(BF16)
    gy = jnp.where(keep_rows(win, slot, cot.shape[1:]), cot[0].astype(F32), 0.0)
    acc_small[0:1] += row_sum(gy)
    gy = gy.astype(BF16)
    acc_out[...] += dot_rows(act, gy)
    grad = dot_back(gy, w_out[...]) * slope
    acc_small[1:2, 0:inner] += row_sum(grad * normed)
    acc_small[1:2, inner : 2 * inner] += row_sum(grad)
    dc = norm_back(grad, normed, inv, g3[...]).astype(BF16)
    dc_out[0] = dc
    acc_small[2:3, 0:inner] += row_sum(dc.astype(F32))
    for tap in range(TAPS):
        acc_conv[tap] += dot_rows(strip[tap * STEP : tap * STEP + rows], dc)

    @pl.when(step == pl.num_programs(0) - 1)
    def _():
        kind = BF16 if last else F32
        gw_conv[...] = acc_conv[...].astype(kind)
        gw_out[...] = acc_out[...].astype(kind)
        small[...] = acc_small[...].astype(kind)


def back_kernel(base, first, last, halves, rows, win, *refs):
    pieces = refs[: 2 * halves + 1]
    refs = refs[2 * halves + 1 :]
    cot, a1, s1, n1, r1, s2, n2, r2, w_conv, g2, w_in, g1 = refs[:12]
    refs = refs[12:]
    if not first:
        win_in, small_in = refs[:2]
        refs = refs[3:]
    grad_out, gw_in, small, acc_in, acc_small, strip = refs
    step = pl.program_id(0)

    @pl.when(step == 0)
    def _():
        if first:
            acc_in[...] = jnp.zeros_like(acc_in)
            acc_small[...] = jnp.zeros_like(acc_small)
        else:
            acc_in[...] = win_in[...]
            acc_small[...] = small_in[...]

    slot = base + step
    at = 0
    for piece in pieces:
        count = piece.shape[1]
        strip[at : at + count] = piece[0]
        at += count
    inner = strip.shape[1]
    width = cot.shape[2]
    dh = dot_back(strip[2 * REACH : 2 * REACH + rows], w_conv[0])
    for tap in range(1, TAPS):
        begin = 2 * REACH - tap * STEP
        dh += dot_back(strip[begin : begin + rows], w_conv[tap])
    dh = jnp.where(keep_rows(win, slot, dh.shape), dh, 0.0).astype(BF16).astype(F32)
    grad = dh * s2[0].astype(F32)
    normed = n2[0].astype(F32)
    acc_small[2:3, 0:inner] += row_sum(grad * normed)
    acc_small[2:3, inner : 2 * inner] += row_sum(grad)
    inv = jnp.concatenate([r2[0]] * (inner // 128), axis=-1)
    dz = norm_back(grad, normed, inv, g2[...]).astype(BF16)
    acc_small[3:4, 0:inner] += row_sum(dz.astype(F32))
    acc_in[...] += dot_rows(a1[0], dz)
    grad = dot_back(dz, w_in[...]) * s1[0].astype(F32)
    normed = n1[0].astype(F32)
    acc_small[0:1] += row_sum(grad * normed)
    acc_small[1:2] += row_sum(grad)
    inv = jnp.concatenate([r1[0]] * (width // 128), axis=-1)
    branch = norm_back(grad, normed, inv, g1[...])
    gy = jnp.where(keep_rows(win, slot, cot.shape[1:]), cot[0].astype(F32), 0.0)
    grad_out[0] = (gy + branch).astype(BF16)

    @pl.when(step == pl.num_programs(0) - 1)
    def _():
        kind = BF16 if last else F32
        gw_in[...] = acc_in[...].astype(kind)
        small[...] = acc_small[...].astype(kind)


def whole(array):
    rank = array.ndim
    return pl.BlockSpec(array.shape, lambda i, w: (0,) * rank, pipeline_mode=pl.Buffered(1))


def per_slot(base, rows, width):
    return pl.BlockSpec((1, rows, width), lambda i, w: (base + i, 0, 0))


def call(kernel, win, args, specs, outs, out_specs, scratch, steps, flops, cost_bytes, aliases, name):
    return pl.pallas_call(
        kernel,
        out_shape=outs,
        grid_spec=pltpu.PrefetchScalarGridSpec(
            num_scalar_prefetch=1,
            grid=(steps,),
            in_specs=specs,
            out_specs=out_specs,
            scratch_shapes=scratch,
        ),
        compiler_params=pltpu.CompilerParams(
            dimension_semantics=("arbitrary",), vmem_limit_bytes=VMEM_LIMIT
        ),
        cost_estimate=pl.CostEstimate(
            flops=flops, bytes_accessed=cost_bytes, transcendentals=0
        ),
        input_output_aliases=aliases,
        name=name,
    )(win, *args)


def front(win, base, steps, tokens, g1, b1, w_in, b_in, g2, b2):
    _, rows, width = tokens.shape
    inner = w_in.shape[1]
    shape = lambda n, kind=BF16: jax.ShapeDtypeStruct((steps, rows, n), kind)
    outs = [shape(inner), shape(width), shape(width), shape(width), shape(128, F32)]
    outs += [shape(inner), shape(inner), shape(128, F32)]
    params = [g1, b1, w_in, b_in, g2, b2]
    return call(
        functools.partial(front_kernel, base),
        win,
        [tokens] + params,
        [per_slot(base, rows, width)] + [whole(p) for p in params],
        outs,
        [per_slot(0, rows, o.shape[2]) for o in outs],
        [],
        steps,
        6 * steps * rows * width * inner,
        steps * rows * width * 12,
        {},
        "front",
    )


def halo(values, hops, axis_size):
    before, after = [], []
    rows = values.shape[1]
    edge = min(rows, REACH)
    for hop in range(1, hops + 1):
        up = [(i, i + hop) for i in range(axis_size - hop)]
        down = [(i + hop, i) for i in range(axis_size - hop)]
        before.insert(0, lax.ppermute(values[:, rows - edge :], "seq", up))
        after.append(lax.ppermute(values[:, :edge], "seq", down))
    return before, after


def rear(win, base, steps, pieces, tokens, cot, params, carry, last):
    _, rows, width = tokens.shape
    w_conv, b_conv, g3, b3, w_out, b_out = params
    inner = w_conv.shape[2]
    halves = len(pieces) // 2
    first = carry is None
    args = list(pieces) + [tokens, cot] + params
    specs = [per_slot(0, p.shape[1], inner) for p in pieces]
    specs += [per_slot(base, rows, width)] * 2 + [whole(p) for p in params]
    aliases = {}
    if not first:
        args += carry[1:] + [carry[0]]
        specs += [whole(c) for c in carry[1:]] + [pl.BlockSpec(memory_space=pl.ANY)]
        aliases = {len(args): 0}
    kind = BF16 if last else F32
    outs = [
        jax.ShapeDtypeStruct(tokens.shape, BF16),
        jax.ShapeDtypeStruct((steps, rows, inner), BF16),
        jax.ShapeDtypeStruct(w_conv.shape, kind),
        jax.ShapeDtypeStruct(w_out.shape, kind),
        jax.ShapeDtypeStruct((8, width), kind),
    ]
    out_specs = [per_slot(base, rows, width), per_slot(0, rows, inner)]
    out_specs += [whole(o) for o in outs[2:]]
    scratch = [
        pltpu.VMEM(w_conv.shape, F32),
        pltpu.VMEM(w_out.shape, F32),
        pltpu.VMEM((8, width), F32),
        pltpu.VMEM((rows + 2 * REACH, inner), BF16),
    ]
    return call(
        functools.partial(rear_kernel, base, first, last, halves, rows),
        win,
        args,
        specs,
        outs,
        out_specs,
        scratch,
        steps,
        2 * steps * rows * inner * (2 * TAPS * inner + 3 * width),
        steps * rows * width * 10,
        aliases,
        "rear",
    )


def back(win, base, steps, pieces, cot, kept, params, carry, last):
    _, rows, width = cot.shape
    w_conv, g2, w_in, g1 = params
    inner = w_conv.shape[2]
    halves = len(pieces) // 2
    first = carry is None
    args = list(pieces) + [cot] + list(kept) + params
    specs = [per_slot(0, p.shape[1], inner) for p in pieces]
    specs += [per_slot(base, rows, width)]
    specs += [per_slot(0, rows, k.shape[2]) for k in kept] + [whole(p) for p in params]
    aliases = {}
    if not first:
        args += carry[1:] + [carry[0]]
        specs += [whole(c) for c in carry[1:]] + [pl.BlockSpec(memory_space=pl.ANY)]
        aliases = {len(args): 0}
    kind = BF16 if last else F32
    outs = [
        jax.ShapeDtypeStruct(cot.shape, BF16),
        jax.ShapeDtypeStruct(w_in.shape, kind),
        jax.ShapeDtypeStruct((8, width), kind),
    ]
    out_specs = [per_slot(base, rows, width)] + [whole(o) for o in outs[1:]]
    scratch = [
        pltpu.VMEM(w_in.shape, F32),
        pltpu.VMEM((8, width), F32),
        pltpu.VMEM((rows + 2 * REACH, inner), BF16),
    ]
    return call(
        functools.partial(back_kernel, base, first, last, halves, rows),
        win,
        args,
        specs,
        outs,
        out_specs,
        scratch,
        steps,
        2 * steps * rows * inner * (TAPS * inner + 2 * width),
        steps * rows * width * 12,
        aliases,
        "back",
    )


def body(
    tokens,
    cotangent,
    ln1_gain,
    ln1_bias,
    w_in,
    b_in,
    ln2_gain,
    ln2_bias,
    w_conv,
    b_conv,
    ln3_gain,
    ln3_bias,
    w_out,
    b_out,
    lengths,
    offsets,
    live,
):
    axis_size = lax.axis_size("seq")
    slots, rows, width = tokens.shape
    inner = w_in.shape[1]
    hops = -(-REACH // rows)
    begin = lax.axis_index("seq") * rows
    filled = jnp.arange(slots, dtype=jnp.int32) < live[0]
    low = jnp.clip(offsets - begin, 0, rows)
    high = jnp.where(filled, jnp.clip(offsets + lengths - begin, 0, rows), 0)
    win = jnp.stack([low, high])
    flat = lambda v: v.astype(F32).reshape(1, -1)
    g1, b1, g2, b2, g3, b3 = map(
        flat, (ln1_gain, ln1_bias, ln2_gain, ln2_bias, ln3_gain, ln3_bias)
    )
    chunks = 2
    steps = slots // chunks
    fronts = [
        front(win, c * steps, steps, tokens, g1, b1, w_in, flat(b_in), g2, b2)
        for c in range(chunks)
    ]
    carry = None
    grads = []
    params = [w_conv, flat(b_conv), g3, b3, w_out, flat(b_out)]
    for c in range(chunks):
        before, after = halo(fronts[c][0], hops, axis_size)
        pieces = before + [fronts[c][0]] + after
        res = rear(
            win, c * steps, steps, pieces, tokens, cotangent, params, carry, c == chunks - 1
        )
        grads.append(res[1])
        carry = [res[0]] + list(res[2:])
    output = carry[0]
    gw_conv, gw_out, small_rear = lax.psum(tuple(carry[1:]), ("dp", "seq"))
    carry = None
    params = [w_conv, g2, w_in, g1]
    for c in range(chunks):
        before, after = halo(grads[c], hops, axis_size)
        pieces = before + [grads[c]] + after
        res = back(
            win, c * steps, steps, pieces, cotangent, fronts[c][1:], params, carry, c == chunks - 1
        )
        carry = list(res)
    grad_tokens = carry[0]
    gw_conv, gw_out, small_rear, late = lax.optimization_barrier(
        (gw_conv, gw_out, small_rear, tuple(carry[1:]))
    )
    gw_in, small_back = lax.psum(late, ("dp", "seq"))
    small_rear = small_rear.astype(F32)
    small_back = small_back.astype(F32)
    return (
        output,
        grad_tokens,
        small_back[0],
        small_back[1],
        gw_in.astype(F32),
        small_back[3, :inner],
        small_back[2, :inner],
        small_back[2, inner : 2 * inner],
        gw_conv.astype(F32),
        small_rear[2, :inner],
        small_rear[1, :inner],
        small_rear[1, inner : 2 * inner],
        gw_out.astype(F32),
        small_rear[0],
    )


def solution(mesh):
    return jax.shard_map(
        body,
        mesh=mesh,
        in_specs=(P("dp", "seq", None),) * 2 + (P(),) * 12 + (P("dp"),) * 3,
        out_specs=(P("dp", "seq", None),) * 2 + (P(),) * 12,
        check_vma=False,
    )
```

time: 1070 us -> 494 us (0.46)
  other arithmetic: 256 us -> 10.5 us
  local copies, waits for them, and re-layouts: 245 us -> 16.2 us
  Pallas kernels: 0 us -> 220 us
  matrix products: 175 us -> 0 us
  waiting for transfers between devices: 171 us -> 90.1 us
  blocking collectives: 176 us -> 114 us
    pallas_call x0 -> x6, Pallas kernels: none -> 220 us  [call(): pl.pallas_call(kernel, out_shape=outs, grid_spec=pltpu.PrefetchScalarGrid...]
    dot_general x9 -> x0, matrix products: 175 us -> none  [the longest x4 78.7 us: row_dot(): return jnp.dot(left, right, preferred_element_type=jnp.float32)]
    all_to_all x4 -> x0, waiting for transfers between devices: 128 us -> none  [the longest x1 76.9 us: body(): lax.all_to_all(deal_shape(tokens, sequence_count), 'seq', split_axis=2, c...]
    reduce_sum x8 -> x0, other arithmetic: 93.1 us -> none  [the longest x1 46.2 us: rear_back(): grad_b_conv = jnp.sum(grad_conv, axis=0, dtype=jnp.float32)]
    unnamed x149 -> x18, local copies, waits for them, and re-layouts: 97.4 us -> 5.01 us
    mul x2 -> x0, other arithmetic: 85.8 us -> none  [the longest x1 56.4 us: normalize(): return (centre * scale_inv, scale_inv)]
    psum x1 -> x2, blocking collectives: 176 us -> 114 us  [the longest x1 74.1 us: body(): gw_conv, gw_out, small_rear = lax.psum(tuple(carry[1:]), ('dp', 'seq'))]
    convert_element_type x17 -> x5, other arithmetic: 69.9 us -> 9.2 us  [the longest x1 3.89 us: body(): gw_conv.astype(F32)]
  transfers between devices with their start and end apart: 5 -> 10, of which waited for: 3 -> 2; matrix products, arithmetic and copies ran while one was open for 35% -> 2% of each run, Pallas kernels for 0% -> 41%
where the time goes in v1:
time: 494 us; the launch traced here: 493 us
  Pallas kernels  220 us (45%)
  blocking collectives  114 us (23%)
  waiting for transfers between devices  90.1 us (18%)
  starting transfers between devices  26.6 us (5%)
  local copies, waits for them, and re-layouts  16.2 us (3%)
  between operations  14.9 us (3%)
  other arithmetic  10.5 us (2%)
    pallas_call x6, Pallas kernels, call(): pl.pallas_call(kernel, out_shape=outs, grid_spec=pltpu.PrefetchScalarGrid...  220 us
    psum x1, waiting for transfers between devices, body(): gw_in, small_back = lax.psum(late, ('dp', 'seq'))  87 us
    psum x1, blocking collectives, body(): gw_conv, gw_out, small_rear = lax.psum(tuple(carry[1:]), ('dp', 'seq'))  74.1 us
    psum x1, blocking collectives, body(): gw_in, small_back = lax.psum(late, ('dp', 'seq'))  40.3 us
    ppermute x4, starting transfers between devices, halo(): before.insert(0, lax.ppermute(values[:, rows - edge:], 'seq', up))  21.2 us
  transfers between devices with their start and end apart: 10, of which 2 were waited for; matrix products, arithmetic and copies ran while one was open for 2% of the time, Pallas kernels for 41%

profile of v1, /device:TPU:0, one launch (start us, length us, event | category | flops | bytes accessed | tf_op | source)
XLA Modules:
  0.0 493.1 jit_solution(2077809295084087821)
XLA Ops:
  7.9 1.3 reshape.99.g2.refs_12_
  9.1 1.3 reshape.97.b_in
  10.4 1.3 reshape.101.b2
  11.7 1.3 reshape.93.g1.refs_14_
  12.9 1.3 reshape.95.b1
  14.2 0.7 clamp_bitcast_fusion
  15.5 19.1 %front.3 = (bf16[8,256,640]{2,1,0:T(8,128)(2,1)}, bf16[8,256,1280]{2,1,0:T(8,128)(2,1)}, bf16[8,256,1280]{2,1,0:T(8,128)(2,1)}, bf16[8,256,1280]{2,1,0:T(8,128)(...) custom-call(s32[2,16]{1,0:T(2,128)} %pad_add_fusion.win, ...), custom_call_target="tpu_custom_call" | custom-call | flops 10066329600 | bytes 31457280 | tf_op jit(solution)/shard_map/front/pallas_call | solution.py:212
  34.7 1.4 collective-permute-start.3
  36.1 4.5 collective-permute-start.2
  40.6 18.9 %front.2 = (bf16[8,256,640]{2,1,0:T(8,128)(2,1)}, bf16[8,256,1280]{2,1,0:T(8,128)(2,1)}, bf16[8,256,1280]{2,1,0:T(8,128)(2,1)}, bf16[8,256,1280]{2,1,0:T(8,128)(...) custom-call(s32[2,16]{1,0:T(2,128)} %pad_add_fusion.win, ...), custom_call_target="tpu_custom_call" | custom-call | flops 10066329600 | bytes 31457280 | tf_op jit(solution)/shard_map/front/pallas_call | solution.py:212
  59.5 1.3 collective-permute-start.1
  60.8 5.2 %collective-permute-start = (bf16[8,256,640]{2,1,0:T(8,128)(2,1)}, bf16[8,256,640]{2,1,0:T(8,128)(2,1)}, u32[]{:S(2)}, u32[]{:S(2)}) collective-permute-start(bf16[8,256,640]{2,1,0:T(8,128)(2,1)} %get-tuple-element.51.refs_1_), channel_id=1, source_target_pairs={{0,1},{1,2},{2,3},{4,5},{5,6},{6,7},{8,9},{9,10},{10,11},{12,13},{... | collective-permute-start | bytes 7864328 | tf_op jit(solution)/shard_map/ppermute | solution.py:263
  68.4 53.1 %rear.2 = (bf16[16,256,1280]{2,1,0:T(8,128)(2,1)}, bf16[8,256,640]{2,1,0:T(8,128)(2,1)}, f32[5,640,640]{2,1,0:T(8,128)}, f32[640,1280]{1,0:T(8,128)}, f32[8,1280]{1,0:T(8,128)}) custom-call(s32[2,16]{1,0:T(2,128)} %pad_add_fusion.win, bf16[8,256,640]{2,1,0:T(8,128)(2,1)} %collective-permute-done.2.refs_0_, bf16[8,256,640]{2,1,0:T(8,128)(2,1)} %get-tuple-element.52.refs_1_, ...), custom_call_target="tpu_custom_call" | custom-call | flops 26843545600 | bytes 26214400 | tf_op jit(solution)/shard_map/rear/pallas_call | solution.py:212
  121.5 1.3 collective-permute-start.7
  122.8 6.2 %collective-permute-start.6 = (bf16[8,256,640]{2,1,0:T(8,128)(2,1)}, bf16[8,256,640]{2,1,0:T(8,128)(2,1)}, u32[]{:S(2)}, u32[]{:S(2)}) collective-permute-start(bf16[8,256,640]{2,1,0:T(8,128)(2,1)} %get-tuple-element.66.refs_1_), channel_id=1, source_target_pairs={{0,1},{1,2},{2,3},{4,5},{5,6},{6,7},{8,9},{9,10},{10,11},{12,13},{... | collective-permute-start | bytes 7864328 | tf_op jit(solution)/shard_map/ppermute | solution.py:263
  129.0 1.5 copy-done.8
  130.5 54.6 %rear.3 = (bf16[16,256,1280]{2,1,0:T(8,128)(2,1)}, bf16[8,256,640]{2,1,0:T(8,128)(2,1)}, bf16[5,640,640]{2,1,0:T(8,128)(2,1)}, bf16[640,1280]{1,0:T(8,128)(2,1)}, bf16[8,1280]{1,0:T(8,128)(2,1)}) custom-call(s32[2,16]{1,0:T(2,128)} %pad_add_fusion.win, bf16[8,256,640]{2,1,0:T(8,128)(2,1)} %collective-permute-done.refs_0_, ...), custom_call_target="tpu_custom_call", output_to_operand_aliasing={{0}: (15, {})} | custom-call | flops 26843545600 | bytes 26214400 | tf_op jit(solution)/shard_map/rear/pallas_call | solution.py:212
  185.1 1.3 collective-permute-start.5
  186.4 5.3 %collective-permute-start.4 = (bf16[8,256,640]{2,1,0:T(8,128)(2,1)}, bf16[8,256,640]{2,1,0:T(8,128)(2,1)}, u32[]{:S(2)}, u32[]{:S(2)}) collective-permute-start(bf16[8,256,640]{2,1,0:T(8,128)(2,1)} %get-tuple-element.58.refs_1_), channel_id=1, source_target_pairs={{0,1},{1,2},{2,3},{4,5},{5,6},{6,7},{8,9},{9,10},{10,11},{12,13},{... | collective-permute-start | bytes 7864328 | tf_op jit(solution)/shard_map/ppermute | solution.py:263
  191.7 0.7 copy-done.3
  192.4 74.1 %psum.37 = bf16[8,1280]{1,0:T(8,128)(2,1)S(1)} all-reduce(bf16[8,1280]{1,0:T(8,128)(2,1)S(1)} %copy-done.3), channel_id=1, replica_groups=mesh['dp'=8,'seq'=4] {'dp','seq'}, use_global_device_ids=true, to_apply=%region_2.3 | all-reduce | flops 10240 | bytes 40960 | tf_op jit(solution)/shard_map/psum | solution.py:407
  266.5 37.1 %back.2 = (bf16[16,256,1280]{2,1,0:T(8,128)(2,1)}, f32[1280,640]{1,0:T(8,128)}, f32[8,1280]{1,0:T(8,128)}) custom-call(s32[2,16]{1,0:T(2,128)} %pad_add_fusion.win, bf16[8,256,640]{2,1,0:T(8,128)(2,1)} %collective-permute-done.6.refs_0_, bf16[8,256,640]{2,1,0:T(8,128)(2,1)} %get-tuple-element.66.refs_1_, ...), custom_call_target="tpu_custom_call" | custom-call | flops 15099494400 | bytes 31457280 | tf_op jit(solution)/shard_map/back/pallas_call | solution.py:212
  303.6 1.5 copy-done.1
  305.1 37.7 %back.3 = (bf16[16,256,1280]{2,1,0:T(8,128)(2,1)}, bf16[1280,640]{1,0:T(8,128)(2,1)}, bf16[8,1280]{1,0:T(8,128)(2,1)}) custom-call(s32[2,16]{1,0:T(2,128)} %pad_add_fusion.win, bf16[8,256,640]{2,1,0:T(8,128)(2,1)} %collective-permute-done.4.refs_0_, bf16[8,256,640]{2,1,0:T(8,128)(2,1)} %get-tuple-element.58.refs_1_, ...), custom_call_target="tpu_custom_call", output_to_operand_aliasing={{0}: (18, {})} | custom-call | flops 15099494400 | bytes 31457280 | tf_op jit(solution)/shard_map/back/pallas_call | solution.py:212
  342.8 3.0 all-reduce.6.cloned.1.call-done
  345.8 40.3 %psum.38 = bf16[8,1280]{1,0:T(8,128)(2,1)S(1)} all-reduce(bf16[8,1280]{1,0:T(8,128)(2,1)} %get-tuple-element.83), channel_id=1, replica_groups=mesh['dp'=8,'seq'=4] {'dp','seq'}, use_global_device_ids=true, to_apply=%region_3.4 | all-reduce | flops 10240 | bytes 40960 | tf_op jit(solution)/shard_map/psum | solution.py:421
  386.2 2.0 convert_element_type.14
  388.1 1.4 copy-done
  389.5 3.9 convert_element_type.12
  395.2 0.6 slice_reduce_fusion.1
  395.9 87.0 %all-reduce.4.cloned.1.call-done = bf16[1280,640]{1,0:T(8,128)(2,1)} async-done(((bf16[1280,640]{1,0:T(8,128)(2,1)}), bf16[1280,640]{1,0:T(8,128)(2,1)}) %all-reduce.4.cloned.1.call-update) | async-done | bytes 1638416 | tf_op jit(solution)/shard_map/psum | solution.py:421
  482.9 3.3 convert_element_type.11
  (36 shorter events, 4.9 us)
Async XLA Ops:
  7.2 338.6 %all-reduce.6.cloned.1.call-start = ((), (), s32[]{:S(2)}) async-start(), calls=%async_computation.1 | async-start | bytes 11468800 | tf_op jit(solution)/shard_map/psum | solution.py:407
  34.6 31.5 %copy-start.5 = (bf16[640]{0:T(1024)(128)(2,1)S(1)}, bf16[640]{0:T(1024)(128)(2,1)}, u32[]{:S(2)}) copy-start(bf16[640]{0:T(1024)(128)(2,1)} %param.26) | copy-start | bytes 3844
  34.6 32.0 %copy-start.6 = (bf16[640]{0:T(1024)(128)(2,1)S(1)}, bf16[640]{0:T(1024)(128)(2,1)}, u32[]{:S(2)}) copy-start(bf16[640]{0:T(1024)(128)(2,1)} %param.27) | copy-start | bytes 3844
  34.6 32.6 %copy-start.7 = (bf16[640]{0:T(1024)(128)(2,1)S(1)}, bf16[640]{0:T(1024)(128)(2,1)}, u32[]{:S(2)}) copy-start(bf16[640]{0:T(1024)(128)(2,1)} %param.28) | copy-start | bytes 3844
  34.6 33.2 %copy-start.4 = (bf16[1280]{0:T(1024)(128)(2,1)S(1)}, bf16[1280]{0:T(1024)(128)(2,1)}, u32[]{:S(2)}) copy-start(bf16[1280]{0:T(1024)(128)(2,1)} %param.30) | copy-start | bytes 7684
  34.7 33.8 %collective-permute-start.3 = (bf16[8,256,640]{2,1,0:T(8,128)(2,1)}, bf16[8,256,640]{2,1,0:T(8,128)(2,1)}, u32[]{:S(2)}, u32[]{:S(2)}) collective-permute-start(bf16[8,256,640]{2,1,0:T(8,128)(2,1)} %get-tuple-element.52.refs_1_), channel_id=1, source_target_pairs={{1,0},{2,1},{3,2},{5,4},{6,5},{7,6},{9,8},{10,9},{11,10},{13,12},{... | collective-permute-start | bytes 7864328 | tf_op jit(solution)/shard_map/ppermute | solution.py:264
  36.1 32.3 %collective-permute-start.2 = (bf16[8,256,640]{2,1,0:T(8,128)(2,1)}, bf16[8,256,640]{2,1,0:T(8,128)(2,1)}, u32[]{:S(2)}, u32[]{:S(2)}) collective-permute-start(bf16[8,256,640]{2,1,0:T(8,128)(2,1)} %get-tuple-element.52.refs_1_), channel_id=1, source_target_pairs={{0,1},{1,2},{2,3},{4,5},{5,6},{6,7},{8,9},{9,10},{10,11},{12,13},{... | collective-permute-start | bytes 7864328 | tf_op jit(solution)/shard_map/ppermute | solution.py:263
  59.5 69.5 %collective-permute-start.1 = (bf16[8,256,640]{2,1,0:T(8,128)(2,1)}, bf16[8,256,640]{2,1,0:T(8,128)(2,1)S(1)}, u32[]{:S(2)}, u32[]{:S(2)}) collective-permute-start(bf16[8,256,640]{2,1,0:T(8,128)(2,1)} %get-tuple-element.51.refs_1_), channel_id=1, source_target_pairs={{1,0},{2,1},{3,2},{5,4},{6,5},{7,6},{9,8},{10,9},{11,10},{13,12},{... | collective-permute-start | bytes 7864328 | tf_op jit(solution)/shard_map/ppermute | solution.py:264
  60.8 68.2 %collective-permute-start = (bf16[8,256,640]{2,1,0:T(8,128)(2,1)}, bf16[8,256,640]{2,1,0:T(8,128)(2,1)}, u32[]{:S(2)}, u32[]{:S(2)}) collective-permute-start(bf16[8,256,640]{2,1,0:T(8,128)(2,1)} %get-tuple-element.51.refs_1_), channel_id=1, source_target_pairs={{0,1},{1,2},{2,3},{4,5},{5,6},{6,7},{8,9},{9,10},{10,11},{12,13},{... | collective-permute-start | bytes 7864328 | tf_op jit(solution)/shard_map/ppermute | solution.py:263
  121.5 145.0 %collective-permute-start.7 = (bf16[8,256,640]{2,1,0:T(8,128)(2,1)}, bf16[8,256,640]{2,1,0:T(8,128)(2,1)}, u32[]{:S(2)}, u32[]{:S(2)}) collective-permute-start(bf16[8,256,640]{2,1,0:T(8,128)(2,1)} %get-tuple-element.66.refs_1_), channel_id=1, source_target_pairs={{1,0},{2,1},{3,2},{5,4},{6,5},{7,6},{9,8},{10,9},{11,10},{13,12},{... | collective-permute-start | bytes 7864328 | tf_op jit(solution)/shard_map/ppermute | solution.py:264
  122.8 143.7 %collective-permute-start.6 = (bf16[8,256,640]{2,1,0:T(8,128)(2,1)}, bf16[8,256,640]{2,1,0:T(8,128)(2,1)}, u32[]{:S(2)}, u32[]{:S(2)}) collective-permute-start(bf16[8,256,640]{2,1,0:T(8,128)(2,1)} %get-tuple-element.66.refs_1_), channel_id=1, source_target_pairs={{0,1},{1,2},{2,3},{4,5},{5,6},{6,7},{8,9},{9,10},{10,11},{12,13},{... | collective-permute-start | bytes 7864328 | tf_op jit(solution)/shard_map/ppermute | solution.py:263
  129.0 1.5 copy-start.8
  185.1 118.5 %collective-permute-start.5 = (bf16[8,256,640]{2,1,0:T(8,128)(2,1)}, bf16[8,256,640]{2,1,0:T(8,128)(2,1)S(1)}, u32[]{:S(2)}, u32[]{:S(2)}) collective-permute-start(bf16[8,256,640]{2,1,0:T(8,128)(2,1)} %get-tuple-element.58.refs_1_), channel_id=1, source_target_pairs={{1,0},{2,1},{3,2},{5,4},{6,5},{7,6},{9,8},{10,9},{11,10},{13,12},{... | collective-permute-start | bytes 7864328 | tf_op jit(solution)/shard_map/ppermute | solution.py:264
  186.4 117.2 %collective-permute-start.4 = (bf16[8,256,640]{2,1,0:T(8,128)(2,1)}, bf16[8,256,640]{2,1,0:T(8,128)(2,1)}, u32[]{:S(2)}, u32[]{:S(2)}) collective-permute-start(bf16[8,256,640]{2,1,0:T(8,128)(2,1)} %get-tuple-element.58.refs_1_), channel_id=1, source_target_pairs={{0,1},{1,2},{2,3},{4,5},{5,6},{6,7},{8,9},{9,10},{10,11},{12,13},{... | collective-permute-start | bytes 7864328 | tf_op jit(solution)/shard_map/ppermute | solution.py:263
  191.6 0.7 copy-start.3
  191.7 291.2 %all-reduce.4.cloned.1.call-start = ((), (), s32[]{:S(2)}) async-start(), calls=%async_computation | async-start | bytes 3276800 | tf_op jit(solution)/shard_map/psum | solution.py:421
  303.6 1.5 copy-start.1
  345.8 40.4 %copy-start.2 = (bf16[640,1280]{1,0:T(8,128)(2,1)S(1)}, bf16[640,1280]{1,0:T(8,128)(2,1)}, u32[]{:S(2)}) copy-start(bf16[640,1280]{1,0:T(8,128)(2,1)} %get-tuple-element.87) | copy-start | bytes 4915204
  386.1 3.3 copy-start
Sparse Core Ops, SparseCore 0:
  191.8 153.9 all-reduce.5
  351.2 131.6 all-reduce.3

commit v2 on v1

--- a/solution.py
+++ b/solution.py
@@ -13,6 +13,7 @@
 EPSILON = 1e-05
 SQRT_HALF = 0.7071067811865476
 INV_ROOT_TAU = 0.3989422804014327
+G1, B1, BIN, G2, B2, BCONV, G3, B3, BOUT = range(9)
 VMEM_LIMIT = 60 * 1024 * 1024
 F32 = jnp.float32
 BF16 = jnp.bfloat16
@@ -64,20 +65,24 @@
     return jnp.broadcast_to(inv, (inv.shape[0], 128))
 
 
-def front_kernel(base, win, tok, g1, b1, w_in, b_in, g2, b2, h, a1, s1, n1, r1, s2, n2, r2):
+def front_kernel(base, win, tok, w_in, table, h, a1, s1, n1, r1, s2, n2, r2):
     slot = base + pl.program_id(0)
+    inner = w_in.shape[1]
+    g1, b1 = table[G1 : G1 + 1], table[B1 : B1 + 1]
+    g2, b2 = table[G2 : G2 + 1, :inner], table[B2 : B2 + 1, :inner]
+    b_in = table[BIN : BIN + 1, :inner]
     normed, inv = normalize(tok[0].astype(F32))
     n1[0] = normed.astype(BF16)
     r1[0] = spread(inv)
-    act, slope = gelu_pair(normed * g1[...] + b1[...])
+    act, slope = gelu_pair(normed * g1 + b1)
     act = act.astype(BF16)
     a1[0] = act
     s1[0] = slope.astype(BF16)
-    hidden = dot(act, w_in[...]) + b_in[...]
+    hidden = dot(act, w_in[...]) + b_in
     normed, inv = normalize(hidden)
     n2[0] = normed.astype(BF16)
     r2[0] = spread(inv)
-    act, slope = gelu_pair(normed * g2[...] + b2[...])
+    act, slope = gelu_pair(normed * g2 + b2)
     s2[0] = slope.astype(BF16)
     h[0] = jnp.where(keep_rows(win, slot, act.shape), act, 0.0).astype(BF16)
 
@@ -87,8 +92,8 @@
 ):
     pieces = refs[: 2 * halves + 1]
     refs = refs[2 * halves + 1 :]
-    tok, cot, w_conv, b_conv, g3, b3, w_out, b_out = refs[:8]
-    refs = refs[8:]
+    tok, cot, w_conv, w_out, table = refs[:5]
+    refs = refs[5:]
     if not first:
         wconv_in, wout_in, small_in = refs[:3]
         refs = refs[4:]
@@ -113,14 +118,16 @@
         strip[at : at + count] = piece[0]
         at += count
     inner = strip.shape[1]
+    g3, b3 = table[G3 : G3 + 1, :inner], table[B3 : B3 + 1, :inner]
+    b_conv, b_out = table[BCONV : BCONV + 1, :inner], table[BOUT : BOUT + 1]
     conv = dot(strip[0:rows], w_conv[0])
     for tap in range(1, TAPS):
         conv += dot(strip[tap * STEP : tap * STEP + rows], w_conv[tap])
-    conv = (conv + b_conv[...]).astype(BF16).astype(F32)
+    conv = (conv + b_conv).astype(BF16).astype(F32)
     normed, inv = normalize(conv)
-    act, slope = gelu_pair(normed * g3[...] + b3[...])
+    act, slope = gelu_pair(normed * g3 + b3)
     act = act.astype(BF16)
-    out[0] = (tok[0].astype(F32) + (dot(act, w_out[...]) + b_out[...])).astype(BF16)
+    out[0] = (tok[0].astype(F32) + (dot(act, w_out[...]) + b_out)).astype(BF16)
     gy = jnp.where(keep_rows(win, slot, cot.shape[1:]), cot[0].astype(F32), 0.0)
     acc_small[0:1] += row_sum(gy)
     gy = gy.astype(BF16)
@@ -128,7 +135,7 @@
     grad = dot_back(gy, w_out[...]) * slope
     acc_small[1:2, 0:inner] += row_sum(grad * normed)
     acc_small[1:2, inner : 2 * inner] += row_sum(grad)
-    dc = norm_back(grad, normed, inv, g3[...]).astype(BF16)
+    dc = norm_back(grad, normed, inv, g3).astype(BF16)
     dc_out[0] = dc
     acc_small[2:3, 0:inner] += row_sum(dc.astype(F32))
     for tap in range(TAPS):
@@ -139,14 +146,14 @@
         kind = BF16 if last else F32
         gw_conv[...] = acc_conv[...].astype(kind)
         gw_out[...] = acc_out[...].astype(kind)
-        small[...] = acc_small[...].astype(kind)
+        small[...] = acc_small[...]
 
 
 def back_kernel(base, first, last, halves, rows, win, *refs):
     pieces = refs[: 2 * halves + 1]
     refs = refs[2 * halves + 1 :]
-    cot, a1, s1, n1, r1, s2, n2, r2, w_conv, g2, w_in, g1 = refs[:12]
-    refs = refs[12:]
+    cot, a1, s1, n1, r1, s2, n2, r2, w_conv, w_in, table = refs[:11]
+    refs = refs[11:]
     if not first:
         win_in, small_in = refs[:2]
         refs = refs[3:]
@@ -169,6 +176,7 @@
         strip[at : at + count] = piece[0]
         at += count
     inner = strip.shape[1]
+    g1, g2 = table[G1 : G1 + 1], table[G2 : G2 + 1, :inner]
     width = cot.shape[2]
     dh = dot_back(strip[2 * REACH : 2 * REACH + rows], w_conv[0])
     for tap in range(1, TAPS):
@@ -180,7 +188,7 @@
     acc_small[2:3, 0:inner] += row_sum(grad * normed)
     acc_small[2:3, inner : 2 * inner] += row_sum(grad)
     inv = jnp.concatenate([r2[0]] * (inner // 128), axis=-1)
-    dz = norm_back(grad, normed, inv, g2[...]).astype(BF16)
+    dz = norm_back(grad, normed, inv, g2).astype(BF16)
     acc_small[3:4, 0:inner] += row_sum(dz.astype(F32))
     acc_in[...] += dot_rows(a1[0], dz)
     grad = dot_back(dz, w_in[...]) * s1[0].astype(F32)
@@ -188,15 +196,20 @@
     acc_small[0:1] += row_sum(grad * normed)
     acc_small[1:2] += row_sum(grad)
     inv = jnp.concatenate([r1[0]] * (width // 128), axis=-1)
-    branch = norm_back(grad, normed, inv, g1[...])
+    branch = norm_back(grad, normed, inv, g1)
     gy = jnp.where(keep_rows(win, slot, cot.shape[1:]), cot[0].astype(F32), 0.0)
     grad_out[0] = (gy + branch).astype(BF16)
 
     @pl.when(step == pl.num_programs(0) - 1)
     def _():
-        kind = BF16 if last else F32
-        gw_in[...] = acc_in[...].astype(kind)
-        small[...] = acc_small[...].astype(kind)
+        if last:
+            depth = acc_in.shape[0] // 16
+            for col in range(inner // 128):
+                part = acc_in[:, col * 128 : (col + 1) * 128].reshape(depth, 16, 128)
+                gw_in[col * depth : (col + 1) * depth] = part.astype(BF16)
+        else:
+            gw_in[...] = acc_in[...]
+        small[...] = acc_small[...]
 
 
 def whole(array):
@@ -230,13 +243,13 @@
     )(win, *args)
 
 
-def front(win, base, steps, tokens, g1, b1, w_in, b_in, g2, b2):
+def front(win, base, steps, tokens, w_in, table):
     _, rows, width = tokens.shape
     inner = w_in.shape[1]
     shape = lambda n, kind=BF16: jax.ShapeDtypeStruct((steps, rows, n), kind)
     outs = [shape(inner), shape(width), shape(width), shape(width), shape(128, F32)]
     outs += [shape(inner), shape(inner), shape(128, F32)]
-    params = [g1, b1, w_in, b_in, g2, b2]
+    params = [w_in, table]
     return call(
         functools.partial(front_kernel, base),
         win,
@@ -267,7 +280,7 @@
 
 def rear(win, base, steps, pieces, tokens, cot, params, carry, last):
     _, rows, width = tokens.shape
-    w_conv, b_conv, g3, b3, w_out, b_out = params
+    w_conv, w_out, _ = params
     inner = w_conv.shape[2]
     halves = len(pieces) // 2
     first = carry is None
@@ -285,7 +298,7 @@
         jax.ShapeDtypeStruct((steps, rows, inner), BF16),
         jax.ShapeDtypeStruct(w_conv.shape, kind),
         jax.ShapeDtypeStruct(w_out.shape, kind),
-        jax.ShapeDtypeStruct((8, width), kind),
+        jax.ShapeDtypeStruct((8, width), F32),
     ]
     out_specs = [per_slot(base, rows, width), per_slot(0, rows, inner)]
     out_specs += [whole(o) for o in outs[2:]]
@@ -313,7 +326,7 @@
 
 def back(win, base, steps, pieces, cot, kept, params, carry, last):
     _, rows, width = cot.shape
-    w_conv, g2, w_in, g1 = params
+    w_conv, w_in, _ = params
     inner = w_conv.shape[2]
     halves = len(pieces) // 2
     first = carry is None
@@ -329,8 +342,8 @@
     kind = BF16 if last else F32
     outs = [
         jax.ShapeDtypeStruct(cot.shape, BF16),
-        jax.ShapeDtypeStruct(w_in.shape, kind),
-        jax.ShapeDtypeStruct((8, width), kind),
+        jax.ShapeDtypeStruct((w_in.size // 2048, 16, 128) if last else w_in.shape, kind),
+        jax.ShapeDtypeStruct((8, width), F32),
     ]
     out_specs = [per_slot(base, rows, width)] + [whole(o) for o in outs[1:]]
     scratch = [
@@ -352,6 +365,127 @@
         aliases,
         "back",
     )
+
+
+def sum_kernel(grid_shape, tiles, gw, small_a, small_b, out, small, mine, got, half, got_x, part, got_d, full, sends, recvs):
+    d_size, x_size = grid_shape
+    seq, dp = lax.axis_index("seq"), lax.axis_index("dp")
+    core, x = lax.rem(seq, 2), lax.div(seq, 2)
+    sibling = {"seq": seq + 1 - 2 * core}
+    x_peers = [{"seq": 2 * lax.rem(x + o, x_size) + core} for o in range(1, x_size)]
+    d_peers = [{"dp": lax.rem(dp + o, d_size)} for o in range(1, d_size)]
+    peers = [sibling] + x_peers + d_peers
+    barrier = pltpu.get_barrier_semaphore()
+    for peer in peers:
+        pl.semaphore_signal(barrier, inc=1, device_id=peer, device_id_type=pl.DeviceIdType.MESH)
+    used = gw.shape[0]
+    mine[0:used] = gw[...]
+    columns = small_a.shape[1] // 128
+    for col in range(columns):
+        lanes = slice(col * 128, (col + 1) * 128)
+        mine[used + col] = jnp.concatenate([small_a[:, lanes], small_b[:, lanes]], axis=0).astype(
+            BF16
+        )
+    spare = mine.shape[0] - used - columns
+    if spare:
+        mine[used + columns :] = jnp.zeros((spare, 16, 128), BF16)
+    pl.semaphore_wait(barrier, len(peers))
+    count = [0]
+
+    def send(src, dst, peer):
+        at = count[0]
+        count[0] += 1
+        copy = pltpu.make_async_remote_copy(
+            src_ref=src,
+            dst_ref=dst,
+            send_sem=sends.at[at],
+            recv_sem=recvs.at[at],
+            device_id=peer,
+            device_id_type=pl.DeviceIdType.MESH,
+        )
+        copy.start()
+        return copy
+
+    x_tiles = d_size * tiles
+    core_tiles = x_size * x_tiles
+    copies = [send(mine.at[pl.ds((1 - core) * core_tiles, core_tiles)], got, sibling)]
+    copies[0].wait_recv()
+    half[...] = (
+        mine[pl.ds(core * core_tiles, core_tiles)].astype(F32) + got[...].astype(F32)
+    ).astype(BF16)
+    now = []
+    for o, peer in enumerate(x_peers):
+        target = lax.rem(x + o + 1, x_size)
+        now.append(send(half.at[pl.ds(target * x_tiles, x_tiles)], got_x.at[o], peer))
+    for copy in now:
+        copy.wait_recv()
+    copies += now
+    total = half[pl.ds(x * x_tiles, x_tiles)].astype(F32)
+    for o in range(x_size - 1):
+        total += got_x[o].astype(F32)
+    part[...] = total.astype(BF16)
+    now = []
+    for o, peer in enumerate(d_peers):
+        target = lax.rem(dp + o + 1, d_size)
+        now.append(send(part.at[pl.ds(target * tiles, tiles)], got_d.at[o], peer))
+    for copy in now:
+        copy.wait_recv()
+    copies += now
+    total = part[pl.ds(dp * tiles, tiles)].astype(F32)
+    for o in range(d_size - 1):
+        total += got_d[o].astype(F32)
+    home_x = core * core_tiles + x * x_tiles
+    own = pl.ds(home_x + dp * tiles, tiles)
+    full[own] = total.astype(BF16)
+    for peers, span in (
+        (d_peers, own),
+        (x_peers, pl.ds(home_x, x_tiles)),
+        ([sibling], pl.ds(core * core_tiles, core_tiles)),
+    ):
+        now = [send(full.at[span], full.at[span], peer) for peer in peers]
+        for copy in now:
+            copy.wait_recv()
+        copies += now
+    for copy in copies:
+        copy.wait_send()
+    depth = out.shape[0] // 16
+    for col in range(out.shape[1] // 128):
+        piece = full[col * depth : (col + 1) * depth].astype(F32)
+        out[:, col * 128 : (col + 1) * 128] = piece.reshape(out.shape[0], 128)
+    for col in range(columns):
+        small[:, col * 128 : (col + 1) * 128] = full[used + col].astype(F32)
+
+
+def sum_all(gw, small_a, small_b, shape):
+    d_size, x_size = lax.axis_size("dp"), lax.axis_size("seq") // 2
+    devices = 2 * d_size * x_size
+    tiles = -(-(gw.shape[0] + small_a.shape[1] // 128) // devices)
+    x_tiles = d_size * tiles
+    copies = 2 * (1 + x_size - 1 + d_size - 1)
+    block = lambda *lead: pltpu.VMEM((*lead, 16, 128), BF16)
+    return pl.pallas_call(
+        functools.partial(sum_kernel, (d_size, x_size), tiles),
+        out_shape=[
+            jax.ShapeDtypeStruct(shape, F32),
+            jax.ShapeDtypeStruct((16, small_a.shape[1]), F32),
+        ],
+        in_specs=[pl.BlockSpec(memory_space=pltpu.VMEM)] * 3,
+        out_specs=[pl.BlockSpec(memory_space=pltpu.VMEM)] * 2,
+        scratch_shapes=[
+            block(devices * tiles),
+            block(x_size * x_tiles),
+            block(x_size * x_tiles),
+            block(x_size - 1, x_tiles),
+            block(x_tiles),
+            block(d_size - 1, tiles),
+            block(devices * tiles),
+            pltpu.SemaphoreType.DMA((copies,)),
+            pltpu.SemaphoreType.DMA((copies,)),
+        ],
+        compiler_params=pltpu.CompilerParams(collective_id=0, has_side_effects=True),
+        cost_estimate=pl.CostEstimate(flops=0, bytes_accessed=120_000_000, transcendentals=0),
+        name="sum_all",
+    )(gw, small_a, small_b)
 
 
 def body(
@@ -382,19 +516,21 @@
     low = jnp.clip(offsets - begin, 0, rows)
     high = jnp.where(filled, jnp.clip(offsets + lengths - begin, 0, rows), 0)
     win = jnp.stack([low, high])
-    flat = lambda v: v.astype(F32).reshape(1, -1)
-    g1, b1, g2, b2, g3, b3 = map(
-        flat, (ln1_gain, ln1_bias, ln2_gain, ln2_bias, ln3_gain, ln3_bias)
+    table = jnp.stack(
+        [
+            jnp.pad(v.astype(F32), (0, width - v.shape[0]))
+            for v in (ln1_gain, ln1_bias, b_in, ln2_gain, ln2_bias, b_conv, ln3_gain, ln3_bias, b_out)
+        ]
     )
     chunks = 2
     steps = slots // chunks
     fronts = [
-        front(win, c * steps, steps, tokens, g1, b1, w_in, flat(b_in), g2, b2)
+        front(win, c * steps, steps, tokens, w_in, table)
         for c in range(chunks)
     ]
     carry = None
     grads = []
-    params = [w_conv, flat(b_conv), g3, b3, w_out, flat(b_out)]
+    params = [w_conv, w_out, table]
     for c in range(chunks):
         before, after = halo(fronts[c][0], hops, axis_size)
         pieces = before + [fronts[c][0]] + after
@@ -404,9 +540,10 @@
         grads.append(res[1])
         carry = [res[0]] + list(res[2:])
     output = carry[0]
-    gw_conv, gw_out, small_rear = lax.psum(tuple(carry[1:]), ("dp", "seq"))
+    gw_conv, gw_out = lax.psum(tuple(carry[1:3]), ("dp", "seq"))
+    small_rear = carry[3]
     carry = None
-    params = [w_conv, g2, w_in, g1]
+    params = [w_conv, w_in, table]
     for c in range(chunks):
         before, after = halo(grads[c], hops, axis_size)
         pieces = before + [grads[c]] + after
@@ -415,18 +552,14 @@
         )
         carry = list(res)
     grad_tokens = carry[0]
-    gw_conv, gw_out, small_rear, late = lax.optimization_barrier(
-        (gw_conv, gw_out, small_rear, tuple(carry[1:]))
-    )
-    gw_in, small_back = lax.psum(late, ("dp", "seq"))
-    small_rear = small_rear.astype(F32)
-    small_back = small_back.astype(F32)
+    gw_in, smalls = sum_all(carry[1], small_rear, carry[2], w_in.shape)
+    small_rear, small_back = smalls[:8], smalls[8:]
     return (
         output,
         grad_tokens,
         small_back[0],
         small_back[1],
-        gw_in.astype(F32),
+        gw_in,
         small_back[3, :inner],
         small_back[2, :inner],
         small_back[2, inner : 2 * inner],

time: 494 us -> 370 us (0.75)
  blocking collectives: 114 us -> 0 us
  waiting for transfers between devices: 90.1 us -> 20.5 us
  Pallas kernels: 220 us -> 282 us
    psum x2 -> x0, blocking collectives: 114 us -> none  [the longest x1 74.1 us: body(): gw_conv, gw_out, small_rear = lax.psum(tuple(carry[1:]), ('dp', 'seq'))]
    psum x2 -> x1, waiting for transfers between devices: 90 us -> 20.5 us  [body(): gw_conv, gw_out = lax.psum(tuple(carry[1:3]), ('dp', 'seq'))]
    pallas_call x0 -> x1, Pallas kernels: none -> 61.3 us  [sum_all(): pl.pallas_call(functools.partial(sum_kernel, (d_size, x_size), tiles), ou...]
    reshape x9 -> x0, local copies, waits for them, and re-layouts: 8.69 us -> none  [body(): flat = lambda v: v.astype(F32).reshape(1, -1)]
  transfers between devices with their start and end apart: 10 -> 9, of which waited for: 2 -> 1; matrix products, arithmetic and copies ran while one was open for 2% -> 1% of each run, Pallas kernels for 41% -> 71%
where the time goes in v2:
time: 370 us; the launch traced here: 369 us
  Pallas kernels  282 us (76%)
  starting transfers between devices  28.7 us (8%)
  waiting for transfers between devices  20.5 us (6%)
  between operations  14.8 us (4%)
  local copies, waits for them, and re-layouts  14 us (4%)
  other arithmetic  9.3 us (3%)
    pallas_call x6, Pallas kernels, call(): pl.pallas_call(kernel, out_shape=outs, grid_spec=pltpu.PrefetchScalarGrid...  220 us
    pallas_call x1, Pallas kernels, sum_all(): pl.pallas_call(functools.partial(sum_kernel, (d_size, x_size), tiles), ou...  61.3 us
    ppermute x4, starting transfers between devices, halo(): before.insert(0, lax.ppermute(values[:, rows - edge:], 'seq', up))  23.5 us
    psum x1, waiting for transfers between devices, body(): gw_conv, gw_out = lax.psum(tuple(carry[1:3]), ('dp', 'seq'))  20.5 us
  transfers between devices with their start and end apart: 9, of which 1 were waited for; matrix products, arithmetic and copies ran while one was open for 1% of the time, Pallas kernels for 71%

profile of v2, /device:TPU:0, one launch (start us, length us, event | category | flops | bytes accessed | tf_op | source)
XLA Modules:
  0.0 368.8 jit_solution(2043487218224570568)
XLA Ops:
  7.9 0.7 pad.25
  8.6 0.7 pad.26
  9.3 0.7 pad.27
  10.0 0.7 pad.28
  10.7 0.7 pad.29
  11.4 0.7 pad.30
  12.1 0.7 stack.53
  12.7 0.7 stack.54
  13.4 0.7 stack.61
  16.1 18.8 %front.3 = (bf16[8,256,640]{2,1,0:T(8,128)(2,1)}, bf16[8,256,1280]{2,1,0:T(8,128)(2,1)}, bf16[8,256,1280]{2,1,0:T(8,128)(2,1)}, bf16[8,256,1280]{2,1,0:T(8,128)(...) custom-call(s32[2,16]{1,0:T(2,128)} %pad_add_fusion.win, ...), custom_call_target="tpu_custom_call" | custom-call | flops 10066329600 | bytes 31457280 | tf_op jit(solution)/shard_map/front/pallas_call | solution.py:225
  34.8 1.3 collective-permute-start.3
  36.1 4.5 %collective-permute-start.2 = (bf16[8,256,640]{2,1,0:T(8,128)(2,1)}, bf16[8,256,640]{2,1,0:T(8,128)(2,1)}, u32[]{:S(2)}, u32[]{:S(2)}) collective-permute-start(bf16[8,256,640]{2,1,0:T(8,128)(2,1)} %get-tuple-element.49.refs_1_), channel_id=1, source_target_pairs={{0,1},{1,2},{2,3},{4,5},{5,6},{6,7},{8,9},{9,10},{10,11},{12,13},{... | collective-permute-start | bytes 7864328 | tf_op jit(solution)/shard_map/ppermute | solution.py:276
  40.7 19.0 %front.2 = (bf16[8,256,640]{2,1,0:T(8,128)(2,1)}, bf16[8,256,1280]{2,1,0:T(8,128)(2,1)}, bf16[8,256,1280]{2,1,0:T(8,128)(2,1)}, bf16[8,256,1280]{2,1,0:T(8,128)(...) custom-call(s32[2,16]{1,0:T(2,128)} %pad_add_fusion.win, ...), custom_call_target="tpu_custom_call" | custom-call | flops 10066329600 | bytes 31457280 | tf_op jit(solution)/shard_map/front/pallas_call | solution.py:225
  59.7 1.3 collective-permute-start.1
  61.0 5.2 %collective-permute-start = (bf16[8,256,640]{2,1,0:T(8,128)(2,1)}, bf16[8,256,640]{2,1,0:T(8,128)(2,1)}, u32[]{:S(2)}, u32[]{:S(2)}) collective-permute-start(bf16[8,256,640]{2,1,0:T(8,128)(2,1)} %get-tuple-element.48.refs_1_), channel_id=1, source_target_pairs={{0,1},{1,2},{2,3},{4,5},{5,6},{6,7},{8,9},{9,10},{10,11},{12,13},{... | collective-permute-start | bytes 7864328 | tf_op jit(solution)/shard_map/ppermute | solution.py:276
  66.2 53.1 %rear.2 = (bf16[16,256,1280]{2,1,0:T(8,128)(2,1)}, bf16[8,256,640]{2,1,0:T(8,128)(2,1)}, f32[5,640,640]{2,1,0:T(8,128)}, f32[640,1280]{1,0:T(8,128)}, f32[8,1280]{1,0:T(8,128)}) custom-call(s32[2,16]{1,0:T(2,128)} %pad_add_fusion.win, bf16[8,256,640]{2,1,0:T(8,128)(2,1)} %collective-permute-done.2.refs_0_, bf16[8,256,640]{2,1,0:T(8,128)(2,1)} %get-tuple-element.49.refs_1_, ...), custom_call_target="tpu_custom_call" | custom-call | flops 26843545600 | bytes 26214400 | tf_op jit(solution)/shard_map/rear/pallas_call | solution.py:225
  119.3 1.3 collective-permute-start.7
  120.6 8.5 %collective-permute-start.6 = (bf16[8,256,640]{2,1,0:T(8,128)(2,1)}, bf16[8,256,640]{2,1,0:T(8,128)(2,1)}, u32[]{:S(2)}, u32[]{:S(2)}) collective-permute-start(bf16[8,256,640]{2,1,0:T(8,128)(2,1)} %get-tuple-element.63.refs_1_), channel_id=1, source_target_pairs={{0,1},{1,2},{2,3},{4,5},{5,6},{6,7},{8,9},{9,10},{10,11},{12,13},{... | collective-permute-start | bytes 7864328 | tf_op jit(solution)/shard_map/ppermute | solution.py:276
  129.2 1.5 copy-done.3
  130.6 54.5 %rear.3 = (bf16[16,256,1280]{2,1,0:T(8,128)(2,1)}, bf16[8,256,640]{2,1,0:T(8,128)(2,1)}, bf16[5,640,640]{2,1,0:T(8,128)(2,1)}, bf16[640,1280]{1,0:T(8,128)(2,1)}, f32[8,1280]{1,0:T(8,128)}) custom-call(s32[2,16]{1,0:T(2,128)} %pad_add_fusion.win, bf16[8,256,640]{2,1,0:T(8,128)(2,1)} %collective-permute-done.refs_0_, ...), custom_call_target="tpu_custom_call", output_to_operand_aliasing={{0}: (12, {})} | custom-call | flops 26843545600 | bytes 26214400 | tf_op jit(solution)/shard_map/rear/pallas_call | solution.py:225
  185.2 1.3 collective-permute-start.5
  186.5 5.3 %collective-permute-start.4 = (bf16[8,256,640]{2,1,0:T(8,128)(2,1)}, bf16[8,256,640]{2,1,0:T(8,128)(2,1)}, u32[]{:S(2)}, u32[]{:S(2)}) collective-permute-start(bf16[8,256,640]{2,1,0:T(8,128)(2,1)} %get-tuple-element.55.refs_1_), channel_id=1, source_target_pairs={{0,1},{1,2},{2,3},{4,5},{5,6},{6,7},{8,9},{9,10},{10,11},{12,13},{... | collective-permute-start | bytes 7864328 | tf_op jit(solution)/shard_map/ppermute | solution.py:276
  191.8 37.1 %back.2 = (bf16[16,256,1280]{2,1,0:T(8,128)(2,1)}, f32[1280,640]{1,0:T(8,128)}, f32[8,1280]{1,0:T(8,128)}) custom-call(s32[2,16]{1,0:T(2,128)} %pad_add_fusion.win, bf16[8,256,640]{2,1,0:T(8,128)(2,1)} %collective-permute-done.6.refs_0_, bf16[8,256,640]{2,1,0:T(8,128)(2,1)} %get-tuple-element.63.refs_1_, ...), custom_call_target="tpu_custom_call" | custom-call | flops 15099494400 | bytes 31457280 | tf_op jit(solution)/shard_map/back/pallas_call | solution.py:225
  228.9 1.5 copy-done.2
  230.3 37.7 %back.3 = (bf16[16,256,1280]{2,1,0:T(8,128)(2,1)}, bf16[400,16,128]{2,1,0:T(8,128)(2,1)}, f32[8,1280]{1,0:T(8,128)}) custom-call(s32[2,16]{1,0:T(2,128)} %pad_add_fusion.win, bf16[8,256,640]{2,1,0:T(8,128)(2,1)} %collective-permute-done.4.refs_0_, bf16[8,256,640]{2,1,0:T(8,128)(2,1)} %get-tuple-element.55.refs_1_, ...), custom_call_target="tpu_custom_call", output_to_operand_aliasing={{0}: (17, {})} | custom-call | flops 15099494400 | bytes 31457280 | tf_op jit(solution)/shard_map/back/pallas_call | solution.py:225
  268.1 61.3 %sum_all.1 = (f32[1280,640]{1,0:T(8,128)}, f32[16,1280]{1,0:T(8,128)}) custom-call(bf16[400,16,128]{2,1,0:T(8,128)(2,1)} %get-tuple-element.75.gw, f32[8,1280]{1,0:T(8,128)} %get-tuple-element.76.small_a, f32[8,1280]{1,0:T(8,128)} %get-tuple-element.77.small_b), custom_call_target="tpu_custom_call" | custom-call | bytes 120000000 | tf_op jit(solution)/shard_map/sum_all/pallas_call | solution.py:466
  329.4 1.5 slice_reduce_fusion
  330.9 1.5 slice_reduce_fusion.3
  332.4 20.5 %all-reduce.9.cloned.1.call-done = (bf16[5,640,640]{2,1,0:T(8,128)(2,1)}, bf16[640,1280]{1,0:T(8,128)(2,1)}) async-done(((bf16[5,640,640]{2,1,0:T(8,128)(2,1)}, bf16[640,1280]{1,0:T(8,128)(2,1)}), (bf16[5,640,640]{2,1,0:T(8,128)(2,1)}, bf16[640,1280]{1,0:T(8,128)(2,1)})) %all-reduce.9.cloned.1.call-update) | async-done | bytes 5734416 | tf_op jit(solution)/shard_map/psum | solution.py:543
  352.9 3.5 convert_element_type.12
  356.4 3.9 %convert_element_type.11 = f32[5,640,640]{2,1,0:T(8,128)} convert(bf16[5,640,640]{2,1,0:T(8,128)(2,1)S(1)} %copy-done) | non-fusion elementwise | flops 2048000 | bytes 12288000 | tf_op jit(solution)/shard_map/convert_element_type | solution.py:566
  360.3 1.7 copy.39
  (26 shorter events, 2.1 us)
Async XLA Ops:
  7.2 345.7 %all-reduce.9.cloned.1.call-start = ((), (), s32[]{:S(2)}) async-start(), calls=%async_computation | async-start | bytes 11468800 | tf_op jit(solution)/shard_map/psum | solution.py:543
  34.8 31.4 %collective-permute-start.3 = (bf16[8,256,640]{2,1,0:T(8,128)(2,1)}, bf16[8,256,640]{2,1,0:T(8,128)(2,1)}, u32[]{:S(2)}, u32[]{:S(2)}) collective-permute-start(bf16[8,256,640]{2,1,0:T(8,128)(2,1)} %get-tuple-element.49.refs_1_), channel_id=1, source_target_pairs={{1,0},{2,1},{3,2},{5,4},{6,5},{7,6},{9,8},{10,9},{11,10},{13,12},{... | collective-permute-start | bytes 7864328 | tf_op jit(solution)/shard_map/ppermute | solution.py:277
  36.1 30.1 %collective-permute-start.2 = (bf16[8,256,640]{2,1,0:T(8,128)(2,1)}, bf16[8,256,640]{2,1,0:T(8,128)(2,1)}, u32[]{:S(2)}, u32[]{:S(2)}) collective-permute-start(bf16[8,256,640]{2,1,0:T(8,128)(2,1)} %get-tuple-element.49.refs_1_), channel_id=1, source_target_pairs={{0,1},{1,2},{2,3},{4,5},{5,6},{6,7},{8,9},{9,10},{10,11},{12,13},{... | collective-permute-start | bytes 7864328 | tf_op jit(solution)/shard_map/ppermute | solution.py:276
  59.7 69.5 %collective-permute-start.1 = (bf16[8,256,640]{2,1,0:T(8,128)(2,1)}, bf16[8,256,640]{2,1,0:T(8,128)(2,1)S(1)}, u32[]{:S(2)}, u32[]{:S(2)}) collective-permute-start(bf16[8,256,640]{2,1,0:T(8,128)(2,1)} %get-tuple-element.48.refs_1_), channel_id=1, source_target_pairs={{1,0},{2,1},{3,2},{5,4},{6,5},{7,6},{9,8},{10,9},{11,10},{13,12},{... | collective-permute-start | bytes 7864328 | tf_op jit(solution)/shard_map/ppermute | solution.py:277
  61.0 68.2 %collective-permute-start = (bf16[8,256,640]{2,1,0:T(8,128)(2,1)}, bf16[8,256,640]{2,1,0:T(8,128)(2,1)}, u32[]{:S(2)}, u32[]{:S(2)}) collective-permute-start(bf16[8,256,640]{2,1,0:T(8,128)(2,1)} %get-tuple-element.48.refs_1_), channel_id=1, source_target_pairs={{0,1},{1,2},{2,3},{4,5},{5,6},{6,7},{8,9},{9,10},{10,11},{12,13},{... | collective-permute-start | bytes 7864328 | tf_op jit(solution)/shard_map/ppermute | solution.py:276
  119.3 72.4 %collective-permute-start.7 = (bf16[8,256,640]{2,1,0:T(8,128)(2,1)}, bf16[8,256,640]{2,1,0:T(8,128)(2,1)}, u32[]{:S(2)}, u32[]{:S(2)}) collective-permute-start(bf16[8,256,640]{2,1,0:T(8,128)(2,1)} %get-tuple-element.63.refs_1_), channel_id=1, source_target_pairs={{1,0},{2,1},{3,2},{5,4},{6,5},{7,6},{9,8},{10,9},{11,10},{13,12},{... | collective-permute-start | bytes 7864328 | tf_op jit(solution)/shard_map/ppermute | solution.py:277
  120.6 71.1 %collective-permute-start.6 = (bf16[8,256,640]{2,1,0:T(8,128)(2,1)}, bf16[8,256,640]{2,1,0:T(8,128)(2,1)}, u32[]{:S(2)}, u32[]{:S(2)}) collective-permute-start(bf16[8,256,640]{2,1,0:T(8,128)(2,1)} %get-tuple-element.63.refs_1_), channel_id=1, source_target_pairs={{0,1},{1,2},{2,3},{4,5},{5,6},{6,7},{8,9},{9,10},{10,11},{12,13},{... | collective-permute-start | bytes 7864328 | tf_op jit(solution)/shard_map/ppermute | solution.py:276
  129.2 1.5 copy-start.3
  185.2 43.7 %collective-permute-start.5 = (bf16[8,256,640]{2,1,0:T(8,128)(2,1)}, bf16[8,256,640]{2,1,0:T(8,128)(2,1)S(1)}, u32[]{:S(2)}, u32[]{:S(2)}) collective-permute-start(bf16[8,256,640]{2,1,0:T(8,128)(2,1)} %get-tuple-element.55.refs_1_), channel_id=1, source_target_pairs={{1,0},{2,1},{3,2},{5,4},{6,5},{7,6},{9,8},{10,9},{11,10},{13,12},{... | collective-permute-start | bytes 7864328 | tf_op jit(solution)/shard_map/ppermute | solution.py:277
  186.5 42.4 %collective-permute-start.4 = (bf16[8,256,640]{2,1,0:T(8,128)(2,1)}, bf16[8,256,640]{2,1,0:T(8,128)(2,1)}, u32[]{:S(2)}, u32[]{:S(2)}) collective-permute-start(bf16[8,256,640]{2,1,0:T(8,128)(2,1)} %get-tuple-element.55.refs_1_), channel_id=1, source_target_pairs={{0,1},{1,2},{2,3},{4,5},{5,6},{6,7},{8,9},{9,10},{10,11},{12,13},{... | collective-permute-start | bytes 7864328 | tf_op jit(solution)/shard_map/ppermute | solution.py:276
  228.9 1.5 copy-start.2
  352.9 3.5 copy-start
  356.4 3.9 %copy-start.1 = (f32[1280,640]{1,0:T(8,128)S(1)}, f32[1280,640]{1,0:T(8,128)}, u32[]{:S(2)}) copy-start(f32[1280,640]{1,0:T(8,128)} %get-tuple-element.113) | copy-start | bytes 9830404
Sparse Core Ops, SparseCore 0:
  191.9 160.9 all-reduce.8

commit v3 on v2

--- a/solution.py
+++ b/solution.py
@@ -71,20 +71,28 @@
     g1, b1 = table[G1 : G1 + 1], table[B1 : B1 + 1]
     g2, b2 = table[G2 : G2 + 1, :inner], table[B2 : B2 + 1, :inner]
     b_in = table[BIN : BIN + 1, :inner]
-    normed, inv = normalize(tok[0].astype(F32))
-    n1[0] = normed.astype(BF16)
-    r1[0] = spread(inv)
-    act, slope = gelu_pair(normed * g1 + b1)
-    act = act.astype(BF16)
-    a1[0] = act
-    s1[0] = slope.astype(BF16)
-    hidden = dot(act, w_in[...]) + b_in
-    normed, inv = normalize(hidden)
-    n2[0] = normed.astype(BF16)
-    r2[0] = spread(inv)
-    act, slope = gelu_pair(normed * g2 + b2)
-    s2[0] = slope.astype(BF16)
-    h[0] = jnp.where(keep_rows(win, slot, act.shape), act, 0.0).astype(BF16)
+    active = win[1, slot] > win[0, slot]
+
+    @pl.when(active)
+    def _():
+        normed, inv = normalize(tok[0].astype(F32))
+        n1[0] = normed.astype(BF16)
+        r1[0] = spread(inv)
+        act, slope = gelu_pair(normed * g1 + b1)
+        act = act.astype(BF16)
+        a1[0] = act
+        s1[0] = slope.astype(BF16)
+        hidden = dot(act, w_in[...]) + b_in
+        normed, inv = normalize(hidden)
+        n2[0] = normed.astype(BF16)
+        r2[0] = spread(inv)
+        act, slope = gelu_pair(normed * g2 + b2)
+        s2[0] = slope.astype(BF16)
+        h[0] = jnp.where(keep_rows(win, slot, act.shape), act, 0.0).astype(BF16)
+
+    @pl.when(jnp.logical_not(active))
+    def _():
+        h[0] = jnp.zeros(h.shape[1:], BF16)
 
 
 def rear_kernel(
@@ -92,12 +100,12 @@
 ):
     pieces = refs[: 2 * halves + 1]
     refs = refs[2 * halves + 1 :]
-    tok, cot, w_conv, w_out, table = refs[:5]
-    refs = refs[5:]
+    cot, w_conv, w_out, table = refs[:4]
+    refs = refs[4:]
     if not first:
         wconv_in, wout_in, small_in = refs[:3]
-        refs = refs[4:]
-    out, dc_out, gw_conv, gw_out, small, acc_conv, acc_out, acc_small, strip = refs
+        refs = refs[3:]
+    a3, dc_out, gw_conv, gw_out, small, acc_conv, acc_out, acc_small, strip = refs
     step = pl.program_id(0)
 
     @pl.when(step == 0)
@@ -119,7 +127,8 @@
         at += count
     inner = strip.shape[1]
     g3, b3 = table[G3 : G3 + 1, :inner], table[B3 : B3 + 1, :inner]
-    b_conv, b_out = table[BCONV : BCONV + 1, :inner], table[BOUT : BOUT + 1]
+    b_conv = table[BCONV : BCONV + 1, :inner]
+
     conv = dot(strip[0:rows], w_conv[0])
     for tap in range(1, TAPS):
         conv += dot(strip[tap * STEP : tap * STEP + rows], w_conv[tap])
@@ -127,19 +136,27 @@
     normed, inv = normalize(conv)
     act, slope = gelu_pair(normed * g3 + b3)
     act = act.astype(BF16)
-    out[0] = (tok[0].astype(F32) + (dot(act, w_out[...]) + b_out)).astype(BF16)
-    gy = jnp.where(keep_rows(win, slot, cot.shape[1:]), cot[0].astype(F32), 0.0)
-    acc_small[0:1] += row_sum(gy)
-    gy = gy.astype(BF16)
-    acc_out[...] += dot_rows(act, gy)
-    grad = dot_back(gy, w_out[...]) * slope
-    acc_small[1:2, 0:inner] += row_sum(grad * normed)
-    acc_small[1:2, inner : 2 * inner] += row_sum(grad)
-    dc = norm_back(grad, normed, inv, g3).astype(BF16)
-    dc_out[0] = dc
-    acc_small[2:3, 0:inner] += row_sum(dc.astype(F32))
-    for tap in range(TAPS):
-        acc_conv[tap] += dot_rows(strip[tap * STEP : tap * STEP + rows], dc)
+    a3[0] = act
+    active = win[1, slot] > win[0, slot]
+
+    @pl.when(active)
+    def _():
+        gy = jnp.where(keep_rows(win, slot, cot.shape[1:]), cot[0].astype(F32), 0.0)
+        acc_small[0:1] += row_sum(gy)
+        gy = gy.astype(BF16)
+        acc_out[...] += dot_rows(act, gy)
+        grad = dot_back(gy, w_out[...]) * slope
+        acc_small[1:2, 0:inner] += row_sum(grad * normed)
+        acc_small[1:2, inner : 2 * inner] += row_sum(grad)
+        dc = norm_back(grad, normed, inv, g3).astype(BF16)
+        dc_out[0] = dc
+        acc_small[2:3, 0:inner] += row_sum(dc.astype(F32))
+        for tap in range(TAPS):
+            acc_conv[tap] += dot_rows(strip[tap * STEP : tap * STEP + rows], dc)
+
+    @pl.when(jnp.logical_not(active))
+    def _():
+        dc_out[0] = jnp.zeros(dc_out.shape[1:], BF16)
 
     @pl.when(step == pl.num_programs(0) - 1)
     def _():
@@ -152,12 +169,12 @@
 def back_kernel(base, first, last, halves, rows, win, *refs):
     pieces = refs[: 2 * halves + 1]
     refs = refs[2 * halves + 1 :]
-    cot, a1, s1, n1, r1, s2, n2, r2, w_conv, w_in, table = refs[:11]
-    refs = refs[11:]
+    tok, cot, a1, s1, n1, r1, s2, n2, r2, a3, w_conv, w_in, w_out, table = refs[:14]
+    refs = refs[14:]
     if not first:
         win_in, small_in = refs[:2]
-        refs = refs[3:]
-    grad_out, gw_in, small, acc_in, acc_small, strip = refs
+        refs = refs[4:]
+    out, grad_out, gw_in, small, acc_in, acc_small, strip = refs
     step = pl.program_id(0)
 
     @pl.when(step == 0)
@@ -178,27 +195,42 @@
     inner = strip.shape[1]
     g1, g2 = table[G1 : G1 + 1], table[G2 : G2 + 1, :inner]
     width = cot.shape[2]
-    dh = dot_back(strip[2 * REACH : 2 * REACH + rows], w_conv[0])
-    for tap in range(1, TAPS):
-        begin = 2 * REACH - tap * STEP
-        dh += dot_back(strip[begin : begin + rows], w_conv[tap])
-    dh = jnp.where(keep_rows(win, slot, dh.shape), dh, 0.0).astype(BF16).astype(F32)
-    grad = dh * s2[0].astype(F32)
-    normed = n2[0].astype(F32)
-    acc_small[2:3, 0:inner] += row_sum(grad * normed)
-    acc_small[2:3, inner : 2 * inner] += row_sum(grad)
-    inv = jnp.concatenate([r2[0]] * (inner // 128), axis=-1)
-    dz = norm_back(grad, normed, inv, g2).astype(BF16)
-    acc_small[3:4, 0:inner] += row_sum(dz.astype(F32))
-    acc_in[...] += dot_rows(a1[0], dz)
-    grad = dot_back(dz, w_in[...]) * s1[0].astype(F32)
-    normed = n1[0].astype(F32)
-    acc_small[0:1] += row_sum(grad * normed)
-    acc_small[1:2] += row_sum(grad)
-    inv = jnp.concatenate([r1[0]] * (width // 128), axis=-1)
-    branch = norm_back(grad, normed, inv, g1)
-    gy = jnp.where(keep_rows(win, slot, cot.shape[1:]), cot[0].astype(F32), 0.0)
-    grad_out[0] = (gy + branch).astype(BF16)
+
+    def residual():
+        sent = dot(a3[0], w_out[...]) + table[BOUT : BOUT + 1]
+        out[0] = (tok[0].astype(F32) + sent).astype(BF16)
+
+    active = win[1, slot] > win[0, slot]
+
+    @pl.when(active)
+    def _():
+        residual()
+        dh = dot_back(strip[2 * REACH : 2 * REACH + rows], w_conv[0])
+        for tap in range(1, TAPS):
+            begin = 2 * REACH - tap * STEP
+            dh += dot_back(strip[begin : begin + rows], w_conv[tap])
+        dh = jnp.where(keep_rows(win, slot, dh.shape), dh, 0.0).astype(BF16).astype(F32)
+        grad = dh * s2[0].astype(F32)
+        normed = n2[0].astype(F32)
+        acc_small[2:3, 0:inner] += row_sum(grad * normed)
+        acc_small[2:3, inner : 2 * inner] += row_sum(grad)
+        inv = jnp.concatenate([r2[0]] * (inner // 128), axis=-1)
+        dz = norm_back(grad, normed, inv, g2).astype(BF16)
+        acc_small[3:4, 0:inner] += row_sum(dz.astype(F32))
+        acc_in[...] += dot_rows(a1[0], dz)
+        grad = dot_back(dz, w_in[...]) * s1[0].astype(F32)
+        normed = n1[0].astype(F32)
+        acc_small[0:1] += row_sum(grad * normed)
+        acc_small[1:2] += row_sum(grad)
+        inv = jnp.concatenate([r1[0]] * (width // 128), axis=-1)
+        branch = norm_back(grad, normed, inv, g1)
+        gy = jnp.where(keep_rows(win, slot, cot.shape[1:]), cot[0].astype(F32), 0.0)
+        grad_out[0] = (gy + branch).astype(BF16)
+
+    @pl.when(jnp.logical_not(active))
+    def _():
+        residual()
+        grad_out[0] = jnp.zeros(grad_out.shape[1:], BF16)
 
     @pl.when(step == pl.num_programs(0) - 1)
     def _():
@@ -278,29 +310,27 @@
     return before, after
 
 
-def rear(win, base, steps, pieces, tokens, cot, params, carry, last):
-    _, rows, width = tokens.shape
+def rear(win, base, steps, pieces, cot, params, carry, last):
+    _, rows, width = cot.shape
     w_conv, w_out, _ = params
     inner = w_conv.shape[2]
     halves = len(pieces) // 2
     first = carry is None
-    args = list(pieces) + [tokens, cot] + params
+    args = list(pieces) + [cot] + params
     specs = [per_slot(0, p.shape[1], inner) for p in pieces]
-    specs += [per_slot(base, rows, width)] * 2 + [whole(p) for p in params]
-    aliases = {}
+    specs += [per_slot(base, rows, width)] + [whole(p) for p in params]
     if not first:
-        args += carry[1:] + [carry[0]]
-        specs += [whole(c) for c in carry[1:]] + [pl.BlockSpec(memory_space=pl.ANY)]
-        aliases = {len(args): 0}
+        args += carry
+        specs += [whole(c) for c in carry]
     kind = BF16 if last else F32
     outs = [
-        jax.ShapeDtypeStruct(tokens.shape, BF16),
+        jax.ShapeDtypeStruct((steps, rows, inner), BF16),
         jax.ShapeDtypeStruct((steps, rows, inner), BF16),
         jax.ShapeDtypeStruct(w_conv.shape, kind),
         jax.ShapeDtypeStruct(w_out.shape, kind),
         jax.ShapeDtypeStruct((8, width), F32),
     ]
-    out_specs = [per_slot(base, rows, width), per_slot(0, rows, inner)]
+    out_specs = [per_slot(0, rows, inner)] * 2
     out_specs += [whole(o) for o in outs[2:]]
     scratch = [
         pltpu.VMEM(w_conv.shape, F32),
@@ -317,35 +347,36 @@
         out_specs,
         scratch,
         steps,
-        2 * steps * rows * inner * (2 * TAPS * inner + 3 * width),
-        steps * rows * width * 10,
-        aliases,
+        2 * steps * rows * inner * (2 * TAPS * inner + 2 * width),
+        steps * rows * width * 6,
+        {},
         "rear",
     )
 
 
-def back(win, base, steps, pieces, cot, kept, params, carry, last):
+def back(win, base, steps, pieces, tokens, cot, kept, params, carry, last):
     _, rows, width = cot.shape
-    w_conv, w_in, _ = params
+    w_conv, w_in, _, _ = params
     inner = w_conv.shape[2]
     halves = len(pieces) // 2
     first = carry is None
-    args = list(pieces) + [cot] + list(kept) + params
+    args = list(pieces) + [tokens, cot] + list(kept) + params
     specs = [per_slot(0, p.shape[1], inner) for p in pieces]
-    specs += [per_slot(base, rows, width)]
+    specs += [per_slot(base, rows, width)] * 2
     specs += [per_slot(0, rows, k.shape[2]) for k in kept] + [whole(p) for p in params]
     aliases = {}
     if not first:
-        args += carry[1:] + [carry[0]]
-        specs += [whole(c) for c in carry[1:]] + [pl.BlockSpec(memory_space=pl.ANY)]
-        aliases = {len(args): 0}
+        args += carry[2:] + carry[:2]
+        specs += [whole(c) for c in carry[2:]] + [pl.BlockSpec(memory_space=pl.ANY)] * 2
+        aliases = {len(args) - 1: 0, len(args): 1}
     kind = BF16 if last else F32
     outs = [
+        jax.ShapeDtypeStruct(cot.shape, BF16),
         jax.ShapeDtypeStruct(cot.shape, BF16),
         jax.ShapeDtypeStruct((w_in.size // 2048, 16, 128) if last else w_in.shape, kind),
         jax.ShapeDtypeStruct((8, width), F32),
     ]
-    out_specs = [per_slot(base, rows, width)] + [whole(o) for o in outs[1:]]
+    out_specs = [per_slot(base, rows, width)] * 2 + [whole(o) for o in outs[2:]]
     scratch = [
         pltpu.VMEM(w_in.shape, F32),
         pltpu.VMEM((8, width), F32),
@@ -360,8 +391,8 @@
         out_specs,
         scratch,
         steps,
-        2 * steps * rows * inner * (TAPS * inner + 2 * width),
-        steps * rows * width * 12,
+        2 * steps * rows * inner * (TAPS * inner + 3 * width),
+        steps * rows * width * 17,
         aliases,
         "back",
     )
@@ -529,30 +560,30 @@
         for c in range(chunks)
     ]
     carry = None
-    grads = []
+    grads, kept = [], []
     params = [w_conv, w_out, table]
     for c in range(chunks):
         before, after = halo(fronts[c][0], hops, axis_size)
         pieces = before + [fronts[c][0]] + after
         res = rear(
-            win, c * steps, steps, pieces, tokens, cotangent, params, carry, c == chunks - 1
+            win, c * steps, steps, pieces, cotangent, params, carry, c == chunks - 1
         )
+        kept.append(list(fronts[c][1:]) + [res[0]])
         grads.append(res[1])
-        carry = [res[0]] + list(res[2:])
-    output = carry[0]
-    gw_conv, gw_out = lax.psum(tuple(carry[1:3]), ("dp", "seq"))
-    small_rear = carry[3]
+        carry = list(res[2:])
+    gw_conv, gw_out = lax.psum(tuple(carry[:2]), ("dp", "seq"))
+    small_rear = carry[2]
     carry = None
-    params = [w_conv, w_in, table]
+    params = [w_conv, w_in, w_out, table]
     for c in range(chunks):
         before, after = halo(grads[c], hops, axis_size)
         pieces = before + [grads[c]] + after
         res = back(
-            win, c * steps, steps, pieces, cotangent, fronts[c][1:], params, carry, c == chunks - 1
+            win, c * steps, steps, pieces, tokens, cotangent, kept[c], params, carry, c == chunks - 1
         )
         carry = list(res)
-    grad_tokens = carry[0]
-    gw_in, smalls = sum_all(carry[1], small_rear, carry[2], w_in.shape)
+    output, grad_tokens = carry[:2]
+    gw_in, smalls = sum_all(carry[2], small_rear, carry[3], w_in.shape)
     small_rear, small_back = smalls[:8], smalls[8:]
     return (
         output,

time: 370 us -> 364 us (0.984)
  waiting for transfers between devices: 20.5 us -> 7.16 us
  starting transfers between devices: 28.7 us -> 33.2 us
    pallas_call x1, Pallas kernels: 61.3 us -> 92 us  [sum_all(): pl.pallas_call(functools.partial(sum_kernel, (d_size, x_size), tiles), ou...]
    pallas_call x6, Pallas kernels: 220 us -> 193 us  [call(): pl.pallas_call(kernel, out_shape=outs, grid_spec=pltpu.PrefetchScalarGrid...]
    psum x1, waiting for transfers between devices: 20.5 us -> 7.13 us  [body(): gw_conv, gw_out = lax.psum(tuple(carry[:2]), ('dp', 'seq'))]
    ppermute x4, starting transfers between devices: 23.5 us -> 28 us  [halo(): before.insert(0, lax.ppermute(values[:, rows - edge:], 'seq', up))]
  transfers between devices with their start and end apart: 9 -> 9, of which waited for: 1 -> 1; matrix products, arithmetic and copies ran while one was open for 1% -> 1% of each run, Pallas kernels for 71% -> 73%
where the time goes in v3:
time: 364 us; the launch traced here: 363 us
  Pallas kernels  285 us (78%)
  starting transfers between devices  33.2 us (9%)
  between operations  14.8 us (4%)
  local copies, waits for them, and re-layouts  14 us (4%)
  other arithmetic  9.32 us (3%)
  waiting for transfers between devices  7.16 us (2%)
    pallas_call x6, Pallas kernels, call(): pl.pallas_call(kernel, out_shape=outs, grid_spec=pltpu.PrefetchScalarGrid...  193 us
    pallas_call x1, Pallas kernels, sum_all(): pl.pallas_call(functools.partial(sum_kernel, (d_size, x_size), tiles), ou...  92 us
    ppermute x4, starting transfers between devices, halo(): before.insert(0, lax.ppermute(values[:, rows - edge:], 'seq', up))  28 us
  transfers between devices with their start and end apart: 9, of which 1 were waited for; matrix products, arithmetic and copies ran while one was open for 1% of the time, Pallas kernels for 73%

profile of v3, /device:TPU:0, one launch (start us, length us, event | category | flops | bytes accessed | tf_op | source)
XLA Modules:
  0.0 363.4 jit_solution(12981696907012558756)
XLA Ops:
  7.9 0.7 pad.25
  8.6 0.7 pad.26
  9.3 0.7 pad.27
  10.0 0.7 pad.28
  10.7 0.7 pad.29
  11.4 0.7 pad.30
  12.1 0.7 stack.53
  12.7 0.7 stack.54
  13.4 0.7 stack.61
  16.1 19.7 %front.3 = (bf16[8,256,640]{2,1,0:T(8,128)(2,1)}, bf16[8,256,1280]{2,1,0:T(8,128)(2,1)}, bf16[8,256,1280]{2,1,0:T(8,128)(2,1)}, bf16[8,256,1280]{2,1,0:T(8,128)(...) custom-call(s32[2,16]{1,0:T(2,128)} %pad_add_fusion.win, ...), custom_call_target="tpu_custom_call" | custom-call | flops 10066329600 | bytes 31457280 | tf_op jit(solution)/shard_map/front/pallas_call | solution.py:257
  35.8 1.3 collective-permute-start.3
  37.1 4.5 %collective-permute-start.2 = (bf16[8,256,640]{2,1,0:T(8,128)(2,1)}, bf16[8,256,640]{2,1,0:T(8,128)(2,1)}, u32[]{:S(2)}, u32[]{:S(2)}) collective-permute-start(bf16[8,256,640]{2,1,0:T(8,128)(2,1)} %get-tuple-element.51.refs_1_), channel_id=1, source_target_pairs={{0,1},{1,2},{2,3},{4,5},{5,6},{6,7},{8,9},{9,10},{10,11},{12,13},{... | collective-permute-start | bytes 7864328 | tf_op jit(solution)/shard_map/ppermute | solution.py:308
  41.6 14.4 %front.2 = (bf16[8,256,640]{2,1,0:T(8,128)(2,1)}, bf16[8,256,1280]{2,1,0:T(8,128)(2,1)}, bf16[8,256,1280]{2,1,0:T(8,128)(2,1)}, bf16[8,256,1280]{2,1,0:T(8,128)(...) custom-call(s32[2,16]{1,0:T(2,128)} %pad_add_fusion.win, ...), custom_call_target="tpu_custom_call" | custom-call | flops 10066329600 | bytes 31457280 | tf_op jit(solution)/shard_map/front/pallas_call | solution.py:257
  56.0 1.3 collective-permute-start.1
  57.3 5.1 %collective-permute-start = (bf16[8,256,640]{2,1,0:T(8,128)(2,1)}, bf16[8,256,640]{2,1,0:T(8,128)(2,1)}, u32[]{:S(2)}, u32[]{:S(2)}) collective-permute-start(bf16[8,256,640]{2,1,0:T(8,128)(2,1)} %get-tuple-element.50.refs_1_), channel_id=1, source_target_pairs={{0,1},{1,2},{2,3},{4,5},{5,6},{6,7},{8,9},{9,10},{10,11},{12,13},{... | collective-permute-start | bytes 7864328 | tf_op jit(solution)/shard_map/ppermute | solution.py:308
  62.4 51.3 %rear.2 = (bf16[8,256,640]{2,1,0:T(8,128)(2,1)}, bf16[8,256,640]{2,1,0:T(8,128)(2,1)}, f32[5,640,640]{2,1,0:T(8,128)}, f32[640,1280]{1,0:T(8,128)}, f32[8,1280]{1,0:T(8,128)}) custom-call(s32[2,16]{1,0:T(2,128)} %pad_add_fusion.win, bf16[8,256,640]{2,1,0:T(8,128)(2,1)} %collective-permute-done.2.refs_0_, bf16[8,256,640]{2,1,0:T(8,128)(2,1)} %get-tuple-element.51.refs_1_, ...), custom_call_target="tpu_custom_call" | custom-call | flops 23488102400 | bytes 15728640 | tf_op jit(solution)/shard_map/rear/pallas_call | solution.py:257
  113.7 1.3 collective-permute-start.7
  115.0 13.2 %collective-permute-start.6 = (bf16[8,256,640]{2,1,0:T(8,128)(2,1)}, bf16[8,256,640]{2,1,0:T(8,128)(2,1)}, u32[]{:S(2)}, u32[]{:S(2)}) collective-permute-start(bf16[8,256,640]{2,1,0:T(8,128)(2,1)} %get-tuple-element.64.refs_1_), channel_id=1, source_target_pairs={{0,1},{1,2},{2,3},{4,5},{5,6},{6,7},{8,9},{9,10},{10,11},{12,13},{... | collective-permute-start | bytes 7864328 | tf_op jit(solution)/shard_map/ppermute | solution.py:308
  128.3 1.5 copy-done.3
  129.8 34.8 %rear.3 = (bf16[8,256,640]{2,1,0:T(8,128)(2,1)}, bf16[8,256,640]{2,1,0:T(8,128)(2,1)}, bf16[5,640,640]{2,1,0:T(8,128)(2,1)}, bf16[640,1280]{1,0:T(8,128)(2,1)}, f32[8,1280]{1,0:T(8,128)}) custom-call(s32[2,16]{1,0:T(2,128)} %pad_add_fusion.win, bf16[8,256,640]{2,1,0:T(8,128)(2,1)} %collective-permute-done.refs_0_, ...), custom_call_target="tpu_custom_call" | custom-call | flops 23488102400 | bytes 15728640 | tf_op jit(solution)/shard_map/rear/pallas_call | solution.py:257
  164.6 1.3 collective-permute-start.5
  165.9 5.2 %collective-permute-start.4 = (bf16[8,256,640]{2,1,0:T(8,128)(2,1)}, bf16[8,256,640]{2,1,0:T(8,128)(2,1)}, u32[]{:S(2)}, u32[]{:S(2)}) collective-permute-start(bf16[8,256,640]{2,1,0:T(8,128)(2,1)} %get-tuple-element.55.refs_1_), channel_id=1, source_target_pairs={{0,1},{1,2},{2,3},{4,5},{5,6},{6,7},{8,9},{9,10},{10,11},{12,13},{... | collective-permute-start | bytes 7864328 | tf_op jit(solution)/shard_map/ppermute | solution.py:308
  171.1 42.2 %back.2 = (bf16[16,256,1280]{2,1,0:T(8,128)(2,1)}, bf16[16,256,1280]{2,1,0:T(8,128)(2,1)}, f32[1280,640]{1,0:T(8,128)}, f32[8,1280]{1,0:T(8,128)}) custom-call(s32[2,16]{1,0:T(2,128)} %pad_add_fusion.win, bf16[8,256,640]{2,1,0:T(8,128)(2,1)} %collective-permute-done.6.refs_0_, bf16[8,256,640]{2,1,0:T(8,128)(2,1)} %get-tuple-element.64.refs_1_, ...), custom_call_target="tpu_custom_call" | custom-call | flops 18454937600 | bytes 44564480 | tf_op jit(solution)/shard_map/back/pallas_call | solution.py:257
  213.3 1.5 copy-done.2
  214.8 30.5 %back.3 = (bf16[16,256,1280]{2,1,0:T(8,128)(2,1)}, bf16[16,256,1280]{2,1,0:T(8,128)(2,1)}, bf16[400,16,128]{2,1,0:T(8,128)(2,1)}, f32[8,1280]{1,0:T(8,128)}) custom-call(s32[2,16]{1,0:T(2,128)} %pad_add_fusion.win, bf16[8,256,640]{2,1,0:T(8,128)(2,1)} %collective-permute-done.4.refs_0_, ...), custom_call_target="tpu_custom_call", output_to_operand_aliasing={{0}: (20, {}), {1}: (21, {})} | custom-call | flops 18454937600 | bytes 44564480 | tf_op jit(solution)/shard_map/back/pallas_call | solution.py:257
  245.2 92.0 %sum_all.1 = (f32[1280,640]{1,0:T(8,128)}, f32[16,1280]{1,0:T(8,128)}) custom-call(bf16[400,16,128]{2,1,0:T(8,128)(2,1)} %get-tuple-element.79.gw, f32[8,1280]{1,0:T(8,128)} %get-tuple-element.80.small_a, f32[8,1280]{1,0:T(8,128)} %get-tuple-element.81.small_b), custom_call_target="tpu_custom_call" | custom-call | bytes 120000000 | tf_op jit(solution)/shard_map/sum_all/pallas_call | solution.py:497
  337.3 1.5 slice_reduce_fusion
  338.8 1.5 slice_reduce_fusion.3
  340.3 7.1 %all-reduce.9.cloned.1.call-done = (bf16[5,640,640]{2,1,0:T(8,128)(2,1)}, bf16[640,1280]{1,0:T(8,128)(2,1)}) async-done(((bf16[5,640,640]{2,1,0:T(8,128)(2,1)}, bf16[640,1280]{1,0:T(8,128)(2,1)}), (bf16[5,640,640]{2,1,0:T(8,128)(2,1)}, bf16[640,1280]{1,0:T(8,128)(2,1)})) %all-reduce.9.cloned.1.call-update) | async-done | bytes 5734416 | tf_op jit(solution)/shard_map/psum | solution.py:574
  347.4 3.5 convert_element_type.12
  350.9 3.9 %convert_element_type.11 = f32[5,640,640]{2,1,0:T(8,128)} convert(bf16[5,640,640]{2,1,0:T(8,128)(2,1)S(1)} %copy-done) | non-fusion elementwise | flops 2048000 | bytes 12288000 | tf_op jit(solution)/shard_map/convert_element_type | solution.py:597
  354.8 1.7 copy.39
  (26 shorter events, 2.1 us)
Async XLA Ops:
  7.2 340.2 %all-reduce.9.cloned.1.call-start = ((), (), s32[]{:S(2)}) async-start(), calls=%async_computation | async-start | bytes 11468800 | tf_op jit(solution)/shard_map/psum | solution.py:574
  35.8 26.6 %collective-permute-start.3 = (bf16[8,256,640]{2,1,0:T(8,128)(2,1)}, bf16[8,256,640]{2,1,0:T(8,128)(2,1)}, u32[]{:S(2)}, u32[]{:S(2)}) collective-permute-start(bf16[8,256,640]{2,1,0:T(8,128)(2,1)} %get-tuple-element.51.refs_1_), channel_id=1, source_target_pairs={{1,0},{2,1},{3,2},{5,4},{6,5},{7,6},{9,8},{10,9},{11,10},{13,12},{... | collective-permute-start | bytes 7864328 | tf_op jit(solution)/shard_map/ppermute | solution.py:309
  37.1 25.3 %collective-permute-start.2 = (bf16[8,256,640]{2,1,0:T(8,128)(2,1)}, bf16[8,256,640]{2,1,0:T(8,128)(2,1)}, u32[]{:S(2)}, u32[]{:S(2)}) collective-permute-start(bf16[8,256,640]{2,1,0:T(8,128)(2,1)} %get-tuple-element.51.refs_1_), channel_id=1, source_target_pairs={{0,1},{1,2},{2,3},{4,5},{5,6},{6,7},{8,9},{9,10},{10,11},{12,13},{... | collective-permute-start | bytes 7864328 | tf_op jit(solution)/shard_map/ppermute | solution.py:308
  56.0 72.3 %collective-permute-start.1 = (bf16[8,256,640]{2,1,0:T(8,128)(2,1)}, bf16[8,256,640]{2,1,0:T(8,128)(2,1)S(1)}, u32[]{:S(2)}, u32[]{:S(2)}) collective-permute-start(bf16[8,256,640]{2,1,0:T(8,128)(2,1)} %get-tuple-element.50.refs_1_), channel_id=1, source_target_pairs={{1,0},{2,1},{3,2},{5,4},{6,5},{7,6},{9,8},{10,9},{11,10},{13,12},{... | collective-permute-start | bytes 7864328 | tf_op jit(solution)/shard_map/ppermute | solution.py:309
  57.3 71.0 %collective-permute-start = (bf16[8,256,640]{2,1,0:T(8,128)(2,1)}, bf16[8,256,640]{2,1,0:T(8,128)(2,1)}, u32[]{:S(2)}, u32[]{:S(2)}) collective-permute-start(bf16[8,256,640]{2,1,0:T(8,128)(2,1)} %get-tuple-element.50.refs_1_), channel_id=1, source_target_pairs={{0,1},{1,2},{2,3},{4,5},{5,6},{6,7},{8,9},{9,10},{10,11},{12,13},{... | collective-permute-start | bytes 7864328 | tf_op jit(solution)/shard_map/ppermute | solution.py:308
  113.7 57.4 %collective-permute-start.7 = (bf16[8,256,640]{2,1,0:T(8,128)(2,1)}, bf16[8,256,640]{2,1,0:T(8,128)(2,1)}, u32[]{:S(2)}, u32[]{:S(2)}) collective-permute-start(bf16[8,256,640]{2,1,0:T(8,128)(2,1)} %get-tuple-element.64.refs_1_), channel_id=1, source_target_pairs={{1,0},{2,1},{3,2},{5,4},{6,5},{7,6},{9,8},{10,9},{11,10},{13,12},{... | collective-permute-start | bytes 7864328 | tf_op jit(solution)/shard_map/ppermute | solution.py:309
  115.0 56.1 %collective-permute-start.6 = (bf16[8,256,640]{2,1,0:T(8,128)(2,1)}, bf16[8,256,640]{2,1,0:T(8,128)(2,1)}, u32[]{:S(2)}, u32[]{:S(2)}) collective-permute-start(bf16[8,256,640]{2,1,0:T(8,128)(2,1)} %get-tuple-element.64.refs_1_), channel_id=1, source_target_pairs={{0,1},{1,2},{2,3},{4,5},{5,6},{6,7},{8,9},{9,10},{10,11},{12,13},{... | collective-permute-start | bytes 7864328 | tf_op jit(solution)/shard_map/ppermute | solution.py:308
  128.3 1.5 copy-start.3
  164.6 48.7 %collective-permute-start.5 = (bf16[8,256,640]{2,1,0:T(8,128)(2,1)}, bf16[8,256,640]{2,1,0:T(8,128)(2,1)S(1)}, u32[]{:S(2)}, u32[]{:S(2)}) collective-permute-start(bf16[8,256,640]{2,1,0:T(8,128)(2,1)} %get-tuple-element.55.refs_1_), channel_id=1, source_target_pairs={{1,0},{2,1},{3,2},{5,4},{6,5},{7,6},{9,8},{10,9},{11,10},{13,12},{... | collective-permute-start | bytes 7864328 | tf_op jit(solution)/shard_map/ppermute | solution.py:309
  165.9 47.4 %collective-permute-start.4 = (bf16[8,256,640]{2,1,0:T(8,128)(2,1)}, bf16[8,256,640]{2,1,0:T(8,128)(2,1)}, u32[]{:S(2)}, u32[]{:S(2)}) collective-permute-start(bf16[8,256,640]{2,1,0:T(8,128)(2,1)} %get-tuple-element.55.refs_1_), channel_id=1, source_target_pairs={{0,1},{1,2},{2,3},{4,5},{5,6},{6,7},{8,9},{9,10},{10,11},{12,13},{... | collective-permute-start | bytes 7864328 | tf_op jit(solution)/shard_map/ppermute | solution.py:308
  213.3 1.5 copy-start.2
  347.4 3.5 copy-start
  350.9 3.9 %copy-start.1 = (f32[1280,640]{1,0:T(8,128)S(1)}, f32[1280,640]{1,0:T(8,128)}, u32[]{:S(2)}) copy-start(f32[1280,640]{1,0:T(8,128)} %get-tuple-element.117) | copy-start | bytes 9830404
Sparse Core Ops, SparseCore 0:
  171.2 176.1 all-reduce.8

commit v4 on v3

--- a/solution.py
+++ b/solution.py
@@ -11,7 +11,8 @@
 STEP = 128
 REACH = (TAPS - 1) // 2 * STEP
 EPSILON = 1e-05
-SQRT_HALF = 0.7071067811865476
+ROOT_TWO = 1.4142135623730951
+EXP_SCALE = -2.8853900817779268
 INV_ROOT_TAU = 0.3989422804014327
 G1, B1, BIN, G2, B2, BCONV, G3, B3, BOUT = range(9)
 VMEM_LIMIT = 60 * 1024 * 1024
@@ -37,10 +38,18 @@
     return centre * inv, inv
 
 
-def gelu_pair(values):
-    gate = 0.5 + 0.5 * lax.erf(values * SQRT_HALF)
-    slope = gate + values * (INV_ROOT_TAU * jnp.exp(-0.5 * values * values))
-    return values * gate, slope
+def gelu_parts(half):
+    rise = 1.0 + lax.erf(half * ROOT_TWO)
+    return half * rise, rise
+
+
+def slope_of(half, rise):
+    return 0.5 * rise + half * (2.0 * INV_ROOT_TAU * jnp.exp2((half * half) * EXP_SCALE))
+
+
+def gelu_pair(half):
+    act, rise = gelu_parts(half)
+    return act, slope_of(half, rise)
 
 
 def norm_back(grad, normed, inv, gain):
@@ -65,7 +74,7 @@
     return jnp.broadcast_to(inv, (inv.shape[0], 128))
 
 
-def front_kernel(base, win, tok, w_in, table, h, a1, s1, n1, r1, s2, n2, r2):
+def front_kernel(base, win, tok, w_in, table, h, a1, n1, r1, s2, n2, r2):
     slot = base + pl.program_id(0)
     inner = w_in.shape[1]
     g1, b1 = table[G1 : G1 + 1], table[B1 : B1 + 1]
@@ -78,15 +87,14 @@
         normed, inv = normalize(tok[0].astype(F32))
         n1[0] = normed.astype(BF16)
         r1[0] = spread(inv)
-        act, slope = gelu_pair(normed * g1 + b1)
+        act, _ = gelu_parts(normed * (0.5 * g1) + 0.5 * b1)
         act = act.astype(BF16)
         a1[0] = act
-        s1[0] = slope.astype(BF16)
         hidden = dot(act, w_in[...]) + b_in
         normed, inv = normalize(hidden)
         n2[0] = normed.astype(BF16)
         r2[0] = spread(inv)
-        act, slope = gelu_pair(normed * g2 + b2)
+        act, slope = gelu_pair(normed * (0.5 * g2) + 0.5 * b2)
         s2[0] = slope.astype(BF16)
         h[0] = jnp.where(keep_rows(win, slot, act.shape), act, 0.0).astype(BF16)
 
@@ -129,12 +137,11 @@
     g3, b3 = table[G3 : G3 + 1, :inner], table[B3 : B3 + 1, :inner]
     b_conv = table[BCONV : BCONV + 1, :inner]
 
-    conv = dot(strip[0:rows], w_conv[0])
-    for tap in range(1, TAPS):
-        conv += dot(strip[tap * STEP : tap * STEP + rows], w_conv[tap])
+    taps = jnp.concatenate([strip[tap * STEP : tap * STEP + rows] for tap in range(TAPS)], axis=1)
+    conv = dot(taps, w_conv[...].reshape(TAPS * inner, inner))
     conv = (conv + b_conv).astype(BF16).astype(F32)
     normed, inv = normalize(conv)
-    act, slope = gelu_pair(normed * g3 + b3)
+    act, slope = gelu_pair(normed * (0.5 * g3) + 0.5 * b3)
     act = act.astype(BF16)
     a3[0] = act
     active = win[1, slot] > win[0, slot]
@@ -169,16 +176,18 @@
 def back_kernel(base, first, last, halves, rows, win, *refs):
     pieces = refs[: 2 * halves + 1]
     refs = refs[2 * halves + 1 :]
-    tok, cot, a1, s1, n1, r1, s2, n2, r2, a3, w_conv, w_in, w_out, table = refs[:14]
-    refs = refs[14:]
+    tok, cot, a1, n1, r1, s2, n2, r2, a3, w_conv, w_in, w_out, table = refs[:13]
+    refs = refs[13:]
     if not first:
         win_in, small_in = refs[:2]
         refs = refs[4:]
-    out, grad_out, gw_in, small, acc_in, acc_small, strip = refs
+    out, grad_out, gw_in, small, acc_in, acc_small, strip, w_flat, slopes = refs
     step = pl.program_id(0)
 
     @pl.when(step == 0)
     def _():
+        for tap in range(TAPS):
+            w_flat[:, tap * strip.shape[1] : (tap + 1) * strip.shape[1]] = w_conv[tap]
         if first:
             acc_in[...] = jnp.zeros_like(acc_in)
             acc_small[...] = jnp.zeros_like(acc_small)
@@ -194,6 +203,7 @@
         at += count
     inner = strip.shape[1]
     g1, g2 = table[G1 : G1 + 1], table[G2 : G2 + 1, :inner]
+    b1 = table[B1 : B1 + 1]
     width = cot.shape[2]
 
     def residual():
@@ -205,10 +215,11 @@
     @pl.when(active)
     def _():
         residual()
-        dh = dot_back(strip[2 * REACH : 2 * REACH + rows], w_conv[0])
-        for tap in range(1, TAPS):
-            begin = 2 * REACH - tap * STEP
-            dh += dot_back(strip[begin : begin + rows], w_conv[tap])
+        half = n1[0].astype(F32) * (0.5 * g1) + 0.5 * b1
+        slopes[...] = slope_of(half, 1.0 + lax.erf(half * ROOT_TWO))
+        begins = [2 * REACH - tap * STEP for tap in range(TAPS)]
+        taps = jnp.concatenate([strip[at : at + rows] for at in begins], axis=1)
+        dh = dot_back(taps, w_flat[...])
         dh = jnp.where(keep_rows(win, slot, dh.shape), dh, 0.0).astype(BF16).astype(F32)
         grad = dh * s2[0].astype(F32)
         normed = n2[0].astype(F32)
@@ -218,7 +229,7 @@
         dz = norm_back(grad, normed, inv, g2).astype(BF16)
         acc_small[3:4, 0:inner] += row_sum(dz.astype(F32))
         acc_in[...] += dot_rows(a1[0], dz)
-        grad = dot_back(dz, w_in[...]) * s1[0].astype(F32)
+        grad = dot_back(dz, w_in[...]) * slopes[...]
         normed = n1[0].astype(F32)
         acc_small[0:1] += row_sum(grad * normed)
         acc_small[1:2] += row_sum(grad)
@@ -279,7 +290,7 @@
     _, rows, width = tokens.shape
     inner = w_in.shape[1]
     shape = lambda n, kind=BF16: jax.ShapeDtypeStruct((steps, rows, n), kind)
-    outs = [shape(inner), shape(width), shape(width), shape(width), shape(128, F32)]
+    outs = [shape(inner), shape(width), shape(width), shape(128, F32)]
     outs += [shape(inner), shape(inner), shape(128, F32)]
     params = [w_in, table]
     return call(
@@ -381,6 +392,8 @@
         pltpu.VMEM(w_in.shape, F32),
         pltpu.VMEM((8, width), F32),
         pltpu.VMEM((rows + 2 * REACH, inner), BF16),
+        pltpu.VMEM((inner, TAPS * inner), BF16),
+        pltpu.VMEM((rows, width), F32),
     ]
     return call(
         functools.partial(back_kernel, base, first, last, halves, rows),

time: 364 us -> 358 us (0.984)
  Pallas kernels: 285 us -> 274 us
  starting transfers between devices: 33.2 us -> 37 us
    pallas_call x6, Pallas kernels: 193 us -> 170 us  [call(): pl.pallas_call(kernel, out_shape=outs, grid_spec=pltpu.PrefetchScalarGrid...]
    pallas_call x1, Pallas kernels: 92 us -> 104 us  [sum_all(): pl.pallas_call(functools.partial(sum_kernel, (d_size, x_size), tiles), ou...]
    ppermute x4, starting transfers between devices: 28 us -> 31.8 us  [halo(): before.insert(0, lax.ppermute(values[:, rows - edge:], 'seq', up))]
  transfers between devices with their start and end apart: 9 -> 9, of which waited for: 1 -> 1; matrix products, arithmetic and copies ran while one was open for 1% -> 1% of each run, Pallas kernels for 73% -> 72%
where the time goes in v4:
time: 358 us; the launch traced here: 357 us
  Pallas kernels  274 us (77%)
  starting transfers between devices  37 us (10%)
  between operations  14.8 us (4%)
  local copies, waits for them, and re-layouts  14 us (4%)
  other arithmetic  9.3 us (3%)
  waiting for transfers between devices  7.87 us (2%)
    pallas_call x6, Pallas kernels, call(): pl.pallas_call(kernel, out_shape=outs, grid_spec=pltpu.PrefetchScalarGrid...  170 us
    pallas_call x1, Pallas kernels, sum_all(): pl.pallas_call(functools.partial(sum_kernel, (d_size, x_size), tiles), ou...  104 us
    ppermute x4, starting transfers between devices, halo(): before.insert(0, lax.ppermute(values[:, rows - edge:], 'seq', up))  31.8 us
    psum x1, waiting for transfers between devices, body(): gw_conv, gw_out = lax.psum(tuple(carry[:2]), ('dp', 'seq'))  7.83 us
  transfers between devices with their start and end apart: 9, of which 1 were waited for; matrix products, arithmetic and copies ran while one was open for 1% of the time, Pallas kernels for 72%

profile of v4, /device:TPU:0, one launch (start us, length us, event | category | flops | bytes accessed | tf_op | source)
XLA Modules:
  0.0 357.3 jit_solution(14643669406054737308)
XLA Ops:
  7.9 0.7 pad.25
  8.6 0.7 pad.26
  9.3 0.7 pad.27
  10.0 0.7 pad.28
  10.7 0.7 pad.29
  11.4 0.7 pad.30
  12.1 0.7 stack.53
  12.7 0.7 stack.54
  13.4 0.7 stack.61
  16.1 16.5 %front.3 = (bf16[8,256,640]{2,1,0:T(8,128)(2,1)}, bf16[8,256,1280]{2,1,0:T(8,128)(2,1)}, bf16[8,256,1280]{2,1,0:T(8,128)(2,1)}, f32[8,256,128]{2,1,0:T(8,128)}, ...) custom-call(s32[2,16]{1,0:T(2,128)} %pad_add_fusion.win, ...), custom_call_target="tpu_custom_call" | custom-call | flops 10066329600 | bytes 31457280 | tf_op jit(solution)/shard_map/front/pallas_call | solution.py:268
  32.6 1.3 collective-permute-start.3
  33.8 4.5 %collective-permute-start.2 = (bf16[8,256,640]{2,1,0:T(8,128)(2,1)}, bf16[8,256,640]{2,1,0:T(8,128)(2,1)}, u32[]{:S(2)}, u32[]{:S(2)}) collective-permute-start(bf16[8,256,640]{2,1,0:T(8,128)(2,1)} %get-tuple-element.49.refs_1_), channel_id=1, source_target_pairs={{0,1},{1,2},{2,3},{4,5},{5,6},{6,7},{8,9},{9,10},{10,11},{12,13},{... | collective-permute-start | bytes 7864328 | tf_op jit(solution)/shard_map/ppermute | solution.py:319
  38.4 10.8 %front.2 = (bf16[8,256,640]{2,1,0:T(8,128)(2,1)}, bf16[8,256,1280]{2,1,0:T(8,128)(2,1)}, bf16[8,256,1280]{2,1,0:T(8,128)(2,1)}, f32[8,256,128]{2,1,0:T(8,128)}, ...) custom-call(s32[2,16]{1,0:T(2,128)} %pad_add_fusion.win, ...), custom_call_target="tpu_custom_call" | custom-call | flops 10066329600 | bytes 31457280 | tf_op jit(solution)/shard_map/front/pallas_call | solution.py:268
  49.1 1.3 collective-permute-start.1
  50.4 5.2 %collective-permute-start = (bf16[8,256,640]{2,1,0:T(8,128)(2,1)}, bf16[8,256,640]{2,1,0:T(8,128)(2,1)}, u32[]{:S(2)}, u32[]{:S(2)}) collective-permute-start(bf16[8,256,640]{2,1,0:T(8,128)(2,1)} %get-tuple-element.48.refs_1_), channel_id=1, source_target_pairs={{0,1},{1,2},{2,3},{4,5},{5,6},{6,7},{8,9},{9,10},{10,11},{12,13},{... | collective-permute-start | bytes 7864328 | tf_op jit(solution)/shard_map/ppermute | solution.py:319
  55.7 47.1 %rear.2 = (bf16[8,256,640]{2,1,0:T(8,128)(2,1)}, bf16[8,256,640]{2,1,0:T(8,128)(2,1)}, f32[5,640,640]{2,1,0:T(8,128)}, f32[640,1280]{1,0:T(8,128)}, f32[8,1280]{1,0:T(8,128)}) custom-call(s32[2,16]{1,0:T(2,128)} %pad_add_fusion.win, bf16[8,256,640]{2,1,0:T(8,128)(2,1)} %collective-permute-done.2.refs_0_, bf16[8,256,640]{2,1,0:T(8,128)(2,1)} %get-tuple-element.49.refs_1_, ...), custom_call_target="tpu_custom_call" | custom-call | flops 23488102400 | bytes 15728640 | tf_op jit(solution)/shard_map/rear/pallas_call | solution.py:268
  102.8 1.3 collective-permute-start.7
  104.1 16.8 %collective-permute-start.6 = (bf16[8,256,640]{2,1,0:T(8,128)(2,1)}, bf16[8,256,640]{2,1,0:T(8,128)(2,1)}, u32[]{:S(2)}, u32[]{:S(2)}) collective-permute-start(bf16[8,256,640]{2,1,0:T(8,128)(2,1)} %get-tuple-element.61.refs_1_), channel_id=1, source_target_pairs={{0,1},{1,2},{2,3},{4,5},{5,6},{6,7},{8,9},{9,10},{10,11},{12,13},{... | collective-permute-start | bytes 7864328 | tf_op jit(solution)/shard_map/ppermute | solution.py:319
  120.9 1.5 copy-done.3
  122.4 27.7 %rear.3 = (bf16[8,256,640]{2,1,0:T(8,128)(2,1)}, bf16[8,256,640]{2,1,0:T(8,128)(2,1)}, bf16[5,640,640]{2,1,0:T(8,128)(2,1)}, bf16[640,1280]{1,0:T(8,128)(2,1)}, f32[8,1280]{1,0:T(8,128)}) custom-call(s32[2,16]{1,0:T(2,128)} %pad_add_fusion.win, bf16[8,256,640]{2,1,0:T(8,128)(2,1)} %collective-permute-done.refs_0_, ...), custom_call_target="tpu_custom_call" | custom-call | flops 23488102400 | bytes 15728640 | tf_op jit(solution)/shard_map/rear/pallas_call | solution.py:268
  150.1 1.3 collective-permute-start.5
  151.4 5.2 %collective-permute-start.4 = (bf16[8,256,640]{2,1,0:T(8,128)(2,1)}, bf16[8,256,640]{2,1,0:T(8,128)(2,1)}, u32[]{:S(2)}, u32[]{:S(2)}) collective-permute-start(bf16[8,256,640]{2,1,0:T(8,128)(2,1)} %get-tuple-element.53.refs_1_), channel_id=1, source_target_pairs={{0,1},{1,2},{2,3},{4,5},{5,6},{6,7},{8,9},{9,10},{10,11},{12,13},{... | collective-permute-start | bytes 7864328 | tf_op jit(solution)/shard_map/ppermute | solution.py:319
  156.7 43.8 %back.2 = (bf16[16,256,1280]{2,1,0:T(8,128)(2,1)}, bf16[16,256,1280]{2,1,0:T(8,128)(2,1)}, f32[1280,640]{1,0:T(8,128)}, f32[8,1280]{1,0:T(8,128)}) custom-call(s32[2,16]{1,0:T(2,128)} %pad_add_fusion.win, bf16[8,256,640]{2,1,0:T(8,128)(2,1)} %collective-permute-done.6.refs_0_, bf16[8,256,640]{2,1,0:T(8,128)(2,1)} %get-tuple-element.61.refs_1_, ...), custom_call_target="tpu_custom_call" | custom-call | flops 18454937600 | bytes 44564480 | tf_op jit(solution)/shard_map/back/pallas_call | solution.py:268
  200.6 1.5 copy-done.2
  202.0 24.5 %back.3 = (bf16[16,256,1280]{2,1,0:T(8,128)(2,1)}, bf16[16,256,1280]{2,1,0:T(8,128)(2,1)}, bf16[400,16,128]{2,1,0:T(8,128)(2,1)}, f32[8,1280]{1,0:T(8,128)}) custom-call(s32[2,16]{1,0:T(2,128)} %pad_add_fusion.win, bf16[8,256,640]{2,1,0:T(8,128)(2,1)} %collective-permute-done.4.refs_0_, ...), custom_call_target="tpu_custom_call", output_to_operand_aliasing={{0}: (19, {}), {1}: (20, {})} | custom-call | flops 18454937600 | bytes 44564480 | tf_op jit(solution)/shard_map/back/pallas_call | solution.py:268
  226.5 103.9 %sum_all.1 = (f32[1280,640]{1,0:T(8,128)}, f32[16,1280]{1,0:T(8,128)}) custom-call(bf16[400,16,128]{2,1,0:T(8,128)(2,1)} %get-tuple-element.75.gw, f32[8,1280]{1,0:T(8,128)} %get-tuple-element.76.small_a, f32[8,1280]{1,0:T(8,128)} %get-tuple-element.77.small_b), custom_call_target="tpu_custom_call" | custom-call | bytes 120000000 | tf_op jit(solution)/shard_map/sum_all/pallas_call | solution.py:510
  330.5 1.5 slice_reduce_fusion
  332.0 1.5 slice_reduce_fusion.3
  333.5 7.8 %all-reduce.9.cloned.1.call-done = (bf16[5,640,640]{2,1,0:T(8,128)(2,1)}, bf16[640,1280]{1,0:T(8,128)(2,1)}) async-done(((bf16[5,640,640]{2,1,0:T(8,128)(2,1)}, bf16[640,1280]{1,0:T(8,128)(2,1)}), (bf16[5,640,640]{2,1,0:T(8,128)(2,1)}, bf16[640,1280]{1,0:T(8,128)(2,1)})) %all-reduce.9.cloned.1.call-update) | async-done | bytes 5734416 | tf_op jit(solution)/shard_map/psum | solution.py:587
  341.3 3.5 convert_element_type.12
  344.8 3.9 %convert_element_type.11 = f32[5,640,640]{2,1,0:T(8,128)} convert(bf16[5,640,640]{2,1,0:T(8,128)(2,1)S(1)} %copy-done) | non-fusion elementwise | flops 2048000 | bytes 12288000 | tf_op jit(solution)/shard_map/convert_element_type | solution.py:610
  348.7 1.7 copy.39
  (26 shorter events, 2.1 us)
Async XLA Ops:
  7.2 334.1 %all-reduce.9.cloned.1.call-start = ((), (), s32[]{:S(2)}) async-start(), calls=%async_computation | async-start | bytes 11468800 | tf_op jit(solution)/shard_map/psum | solution.py:587
  32.6 23.1 %collective-permute-start.3 = (bf16[8,256,640]{2,1,0:T(8,128)(2,1)}, bf16[8,256,640]{2,1,0:T(8,128)(2,1)}, u32[]{:S(2)}, u32[]{:S(2)}) collective-permute-start(bf16[8,256,640]{2,1,0:T(8,128)(2,1)} %get-tuple-element.49.refs_1_), channel_id=1, source_target_pairs={{1,0},{2,1},{3,2},{5,4},{6,5},{7,6},{9,8},{10,9},{11,10},{13,12},{... | collective-permute-start | bytes 7864328 | tf_op jit(solution)/shard_map/ppermute | solution.py:320
  33.8 21.8 %collective-permute-start.2 = (bf16[8,256,640]{2,1,0:T(8,128)(2,1)}, bf16[8,256,640]{2,1,0:T(8,128)(2,1)}, u32[]{:S(2)}, u32[]{:S(2)}) collective-permute-start(bf16[8,256,640]{2,1,0:T(8,128)(2,1)} %get-tuple-element.49.refs_1_), channel_id=1, source_target_pairs={{0,1},{1,2},{2,3},{4,5},{5,6},{6,7},{8,9},{9,10},{10,11},{12,13},{... | collective-permute-start | bytes 7864328 | tf_op jit(solution)/shard_map/ppermute | solution.py:319
  49.1 71.7 %collective-permute-start.1 = (bf16[8,256,640]{2,1,0:T(8,128)(2,1)}, bf16[8,256,640]{2,1,0:T(8,128)(2,1)S(1)}, u32[]{:S(2)}, u32[]{:S(2)}) collective-permute-start(bf16[8,256,640]{2,1,0:T(8,128)(2,1)} %get-tuple-element.48.refs_1_), channel_id=1, source_target_pairs={{1,0},{2,1},{3,2},{5,4},{6,5},{7,6},{9,8},{10,9},{11,10},{13,12},{... | collective-permute-start | bytes 7864328 | tf_op jit(solution)/shard_map/ppermute | solution.py:320
  50.4 70.4 %collective-permute-start = (bf16[8,256,640]{2,1,0:T(8,128)(2,1)}, bf16[8,256,640]{2,1,0:T(8,128)(2,1)}, u32[]{:S(2)}, u32[]{:S(2)}) collective-permute-start(bf16[8,256,640]{2,1,0:T(8,128)(2,1)} %get-tuple-element.48.refs_1_), channel_id=1, source_target_pairs={{0,1},{1,2},{2,3},{4,5},{5,6},{6,7},{8,9},{9,10},{10,11},{12,13},{... | collective-permute-start | bytes 7864328 | tf_op jit(solution)/shard_map/ppermute | solution.py:319
  102.8 53.9 %collective-permute-start.7 = (bf16[8,256,640]{2,1,0:T(8,128)(2,1)}, bf16[8,256,640]{2,1,0:T(8,128)(2,1)}, u32[]{:S(2)}, u32[]{:S(2)}) collective-permute-start(bf16[8,256,640]{2,1,0:T(8,128)(2,1)} %get-tuple-element.61.refs_1_), channel_id=1, source_target_pairs={{1,0},{2,1},{3,2},{5,4},{6,5},{7,6},{9,8},{10,9},{11,10},{13,12},{... | collective-permute-start | bytes 7864328 | tf_op jit(solution)/shard_map/ppermute | solution.py:320
  104.1 52.6 %collective-permute-start.6 = (bf16[8,256,640]{2,1,0:T(8,128)(2,1)}, bf16[8,256,640]{2,1,0:T(8,128)(2,1)}, u32[]{:S(2)}, u32[]{:S(2)}) collective-permute-start(bf16[8,256,640]{2,1,0:T(8,128)(2,1)} %get-tuple-element.61.refs_1_), channel_id=1, source_target_pairs={{0,1},{1,2},{2,3},{4,5},{5,6},{6,7},{8,9},{9,10},{10,11},{12,13},{... | collective-permute-start | bytes 7864328 | tf_op jit(solution)/shard_map/ppermute | solution.py:319
  120.9 1.5 copy-start.3
  150.1 50.4 %collective-permute-start.5 = (bf16[8,256,640]{2,1,0:T(8,128)(2,1)}, bf16[8,256,640]{2,1,0:T(8,128)(2,1)S(1)}, u32[]{:S(2)}, u32[]{:S(2)}) collective-permute-start(bf16[8,256,640]{2,1,0:T(8,128)(2,1)} %get-tuple-element.53.refs_1_), channel_id=1, source_target_pairs={{1,0},{2,1},{3,2},{5,4},{6,5},{7,6},{9,8},{10,9},{11,10},{13,12},{... | collective-permute-start | bytes 7864328 | tf_op jit(solution)/shard_map/ppermute | solution.py:320
  151.4 49.1 %collective-permute-start.4 = (bf16[8,256,640]{2,1,0:T(8,128)(2,1)}, bf16[8,256,640]{2,1,0:T(8,128)(2,1)}, u32[]{:S(2)}, u32[]{:S(2)}) collective-permute-start(bf16[8,256,640]{2,1,0:T(8,128)(2,1)} %get-tuple-element.53.refs_1_), channel_id=1, source_target_pairs={{0,1},{1,2},{2,3},{4,5},{5,6},{6,7},{8,9},{9,10},{10,11},{12,13},{... | collective-permute-start | bytes 7864328 | tf_op jit(solution)/shard_map/ppermute | solution.py:319
  200.5 1.5 copy-start.2
  341.3 3.5 copy-start
  344.8 3.9 %copy-start.1 = (f32[1280,640]{1,0:T(8,128)S(1)}, f32[1280,640]{1,0:T(8,128)}, u32[]{:S(2)}) copy-start(f32[1280,640]{1,0:T(8,128)} %get-tuple-element.113) | copy-start | bytes 9830404
Sparse Core Ops, SparseCore 0:
  156.8 184.4 all-reduce.8
